TPU v7x, 512 devices: a whole 4x8x8 slice. The times are simulated.
512 devices in a mesh: lon: 64 (over z_lo, y, core), plane: 8 (over z_hi, x).
Axes of the slice: x: 4, y: 8, z: 8 (z_hi: 2, z_lo: 4; z = z_hi * 4 + z_lo), core: 2. Of those that a mesh axis runs over, the one named last changes fastest.
Arguments:
- potential: float32 [8, 256, 16384], P('plane', None, 'lon'), may hold values from -0.6 to 0.6
- lens_weight: float32 [8, 8], P('plane'), may hold values from 0.1 to 0.3
- cycle_shift: int32 [2, 256], replicated, may hold values from -3 to 2
- cycle_weight: int32 [2, 256], replicated, may hold values from 0 to 16
- cycle_scale: float32 [256], replicated, may hold values from 1 to 2
Outputs:
- displacement: float32 [8, 2, 256, 16384], P('plane', None, None, 'lon')
- jacobian: float32 [8, 4, 256, 16384], P('plane', None, None, 'lon')
All inputs are finite; a program needn't handle non-finite values.
Results may differ from a plain program's by a relative error of at most 0.00002.
Values sent between devices are 32-bit elements; how exact they have to be, the bound alone decides.
No kernel may reach another device: no remote copies, remote signals or barrier semaphores. Data moves between devices by JAX's collectives and lax.ppermute only.
A program may use at most 64 MiB of HBM per device.

v0:
```python
import jax
import jax.numpy as jnp
from jax import lax
from jax.sharding import PartitionSpec as P

HALO = 4


def shifted(value, axis, steps):
    count = lax.axis_size(axis)
    pairs = [(source, (source + steps) % count) for source in range(count)]
    return lax.ppermute(value, axis, pairs)


def extended(block, sides, width):
    for axis, dim in sides:
        count = lax.axis_size(axis)
        forward = [(i, i + 1) for i in range(count - 1)]
        forward.append((count - 1, 0))
        backward = [(target, source) for source, target in forward]
        low = lax.ppermute(
            lax.slice_in_dim(block, block.shape[dim] - width, None, axis=dim), axis, forward
        )
        high = lax.ppermute(lax.slice_in_dim(block, 0, width, axis=dim), axis, backward)
        block = jnp.concatenate([low, block, high], axis=dim)
    return block


def from_root(shard, axis, root):
    mine = lax.axis_index(axis) == root
    return lax.psum(jnp.where(mine, shard, jnp.zeros_like(shard)), axis)


def pick_cycle(row_block, shifts, offset, width):
    result = jnp.zeros((row_block.shape[0], width), jnp.float32)
    for delta in range(-3, 3):
        start = HALO + delta + offset
        result = jnp.where(shifts[:, None] == delta, row_block[:, start : start + width], result)
    return result


def cycle_value(row_block, shifts, weights, offset, width):
    frac = weights.astype(jnp.float32)[:, None] / 16.0
    first = pick_cycle(row_block, shifts, offset, width)
    second = pick_cycle(row_block, shifts, offset + 1, width)
    return (1.0 - frac) * first + frac * second


def derivatives(padded, cycle_shift, cycle_weight, cycle_scale):
    width = padded.shape[1] - 2 * HALO
    north_rows = padded[:-2]
    south_rows = padded[2:]
    middle = padded[1:-1]
    north = [
        cycle_value(north_rows, cycle_shift[0], cycle_weight[0], offset, width)
        for offset in (-1, 0, 1)
    ]
    south = [
        cycle_value(south_rows, cycle_shift[1], cycle_weight[1], offset, width)
        for offset in (-1, 0, 1)
    ]
    center = [middle[:, HALO + offset : HALO + offset + width] for offset in (-1, 0, 1)]
    metric = cycle_scale[:, None]
    alpha_t = 0.5 * (south[1] - north[1])
    alpha_p = 0.5 * metric * (center[2] - center[0])
    shear_tt = south[1] - 2.0 * center[1] + north[1]
    shear_pp = metric * metric * (center[2] - 2.0 * center[1] + center[0])
    shear_tp = 0.25 * metric * (south[2] - south[0] - north[2] + north[0])
    return (alpha_t, alpha_p, shear_tt, shear_pp, shear_tp)


def advance(state, fields, gain):
    disp_t, disp_p, a_zz, a_zo, a_oz, a_oo = state
    alpha_t, alpha_p, shear_tt, shear_pp, shear_tp = fields
    new_t = disp_t - gain * (alpha_t + shear_tt * disp_t + shear_tp * disp_p)
    new_p = disp_p - gain * (alpha_p + shear_tp * disp_t + shear_pp * disp_p)
    b_zz = a_zz - gain * (shear_tt * a_zz + shear_tp * a_oz)
    b_zo = a_zo - gain * (shear_tt * a_zo + shear_tp * a_oo)
    b_oz = a_oz - gain * (shear_tp * a_zz + shear_pp * a_oz)
    b_oo = a_oo - gain * (shear_tp * a_zo + shear_pp * a_oo)
    return (new_t, new_p, b_zz, b_zo, b_oz, b_oo)


def pad_rows(tile):
    return jnp.pad(tile, ((1, 1), (0, 0)))


def per_device(potential, lens_weight, cycle_shift, cycle_weight, cycle_scale):
    planes = lax.axis_size("plane")
    lon_count = lax.axis_size("lon")
    by_tiles = lon_count - lon_count // 4
    rows_count = potential.shape[1]
    width = potential.shape[2]
    gains = lens_weight[0]
    zeros = jnp.zeros((rows_count, width), jnp.float32)
    ones = jnp.ones((rows_count, width), jnp.float32)
    state = (zeros, zeros, ones, zeros, zeros, ones)
    for plane_k in range(planes):
        turned = shifted(from_root(potential, "plane", plane_k), "lon", by_tiles)
        sky_tile = extended(turned, (("lon", 2),), HALO)[0]
        fields = derivatives(pad_rows(sky_tile), cycle_shift, cycle_weight, cycle_scale)
        state = advance(state, fields, gains[plane_k])
    displacement = jnp.stack(state[0:2])[None]
    jacobian = jnp.stack(state[2:6])[None]
    return (displacement, jacobian)


def solution(mesh):
    in_specs = (P("plane", None, "lon"), P("plane", None), P(), P(), P())
    out_specs = (P("plane", None, None, "lon"), P("plane", None, None, "lon"))
    return jax.shard_map(
        per_device, mesh=mesh, in_specs=in_specs, out_specs=out_specs, check_vma=False
    )
```

profile of v0, /device:TPU:6, one launch (start us, length us, event | category | flops | bytes accessed | tf_op | source)
XLA Modules:
  0.0 324.3 jit_solution(139829288068550160)
XLA Ops:
  7.2 2.3 broadcast_select_fusion
  9.5 0.7 copy-done.1
  10.2 0.7 copy-done.3
  10.9 149.9 %all-reduce.11.cloned.1.call-done = (f32[1,256,256]{2,1,0:T(8,128)}, f32[1,256,256]{2,1,0:T(8,128)}, f32[1,256,256]{2,1,0:T(8,128)}, f32[1,256,256]{2,1,0:T(8,12...) async-done(((f32[1,256,256]{2,1,0:T(8,128)}, f32[1,256,256]{2,1,0:T(8,128)}, f32[1,256,256]{2,1,0:T(8,128)}, ...) | async-done | bytes 2097168 | tf_op jit(solution)/shard_map/psum | solution.py:31
  160.8 1.9 collective-permute-start
  162.7 0.7 copy-done.2
  163.5 1.9 collective-permute-start.3
  165.4 0.7 fusion.8
  166.1 1.9 collective-permute-start.6
  168.0 6.8 %collective-permute-start.9 = (f32[1,256,256]{2,1,0:T(8,128)}, f32[1,256,256]{2,1,0:T(8,128)S(1)}, u32[]{:S(2)}, u32[]{:S(2)}) collective-permute-start(f32[1,256,256]{2,1,0:T(8,128)} %get-tuple-element.17), channel_id=1, source_target_pairs={{0,384},{8,392},{16,400},{24,408},{32,416},{40,424},{48,432},{56,4... | collective-permute-start | bytes 786440 | tf_op jit(solution)/shard_map/ppermute | solution.py:12
  174.8 1.9 collective-permute-start.12
  176.8 2.1 collective-permute-start.15
  178.8 0.1 fusion.3
  179.0 2.5 collective-permute-start.18
  181.5 0.1 fusion.4
  181.6 1.7 collective-permute-done.6
  183.3 4.7 %collective-permute-start.21 = (f32[1,256,256]{2,1,0:T(8,128)S(1)}, f32[1,256,256]{2,1,0:T(8,128)S(1)}, u32[]{:S(2)}, u32[]{:S(2)}) collective-permute-start(f32[1,256,256]{2,1,0:T(8,128)S(1)} %copy-done.4), channel_id=1, source_target_pairs={{0,384},{8,392},{16,400},{24,408},{32,416},{40,424},{48,432},{56,4... | collective-permute-start | bytes 786440 | tf_op jit(solution)/shard_map/ppermute | solution.py:12
  188.0 0.1 fusion.2
  188.1 0.8 collective-permute-done.9
  188.9 1.9 collective-permute-start.1
  190.9 3.6 %collective-permute-done.12 = f32[1,256,256]{2,1,0:T(8,128)S(1)} collective-permute-done((f32[1,256,256]{2,1,0:T(8,128)}, f32[1,256,256]{2,1,0:T(8,128)S(1)}, u32[]{:S(2)}, u32[]{:S(2)}) %collective-permute-start.12) | collective-permute-done | bytes 262176 | tf_op jit(solution)/shard_map/ppermute | solution.py:12
  194.5 4.0 %collective-permute-start.2 = (f32[1,256,4]{2,1,0:T(8,128)S(1)}, f32[1,256,4]{2,1,0:T(8,128)S(1)}, u32[]{:S(2)}, u32[]{:S(2)}) collective-permute-start(f32[1,256,4]{2,1,0:T(8,128)S(1)} %get-tuple-element.114), channel_id=1, source_target_pairs={{8,0},{16,8},{24,16},{32,24},{40,32},{48,40},{56,48},{64,56},{72,6... | collective-permute-start | bytes 12296 | tf_op jit(solution)/shard_map/ppermute | solution.py:24
  198.6 3.0 collective-permute-done.15
  201.5 1.9 collective-permute-start.4
  203.5 4.5 %collective-permute-done.18 = f32[1,256,256]{2,1,0:T(8,128)S(1)} collective-permute-done((f32[1,256,256]{2,1,0:T(8,128)S(1)}, f32[1,256,256]{2,1,0:T(8,128)S(1)}, u32[]{:S(2)}, u32[]{:S(2)}) %collective-permute-start.18) | collective-permute-done | bytes 262176 | tf_op jit(solution)/shard_map/ppermute | solution.py:12
  208.0 3.1 collective-permute-start.5
  211.2 1.0 collective-permute-done.21
  212.2 1.9 collective-permute-start.7
  214.2 7.5 %collective-permute-start.8 = (f32[1,256,4]{2,1,0:T(8,128)S(1)}, f32[1,256,4]{2,1,0:T(8,128)S(1)}, u32[]{:S(2)}, u32[]{:S(2)}) collective-permute-start(f32[1,256,4]{2,1,0:T(8,128)S(1)} %get-tuple-element.112), channel_id=1, source_target_pairs={{8,0},{16,8},{24,16},{32,24},{40,32},{48,40},{56,48},{64,56},{72,6... | collective-permute-start | bytes 12296 | tf_op jit(solution)/shard_map/ppermute | solution.py:24
  221.8 1.9 collective-permute-start.10
  223.7 0.2 maximum_bitcast_fusion.2
  224.0 7.5 %collective-permute-start.11 = (f32[1,256,4]{2,1,0:T(8,128)S(1)}, f32[1,256,4]{2,1,0:T(8,128)S(1)}, u32[]{:S(2)}, u32[]{:S(2)}) collective-permute-start(f32[1,256,4]{2,1,0:T(8,128)S(1)} %get-tuple-element.118), channel_id=1, source_target_pairs={{8,0},{16,8},{24,16},{32,24},{40,32},{48,40},{56,48},{64,56},{72,6... | collective-permute-start | bytes 12296 | tf_op jit(solution)/shard_map/ppermute | solution.py:24
  231.5 1.9 collective-permute-start.13
  233.5 0.2 maximum_bitcast_fusion.3
  233.7 6.8 %multiply_subtract_fusion.25 = (f32[256,256]{1,0:T(8,128)S(1)}, f32[256,256]{1,0:T(8,128)S(1)}, f32[256,256]{1,0:T(8,128)S(1)}, f32[256,256]{1,0:T(8,128)S(1)}, ...) fusion(f32[]{:T(128)} %bitcast.4, f32[]{:T(128)} %bitcast, ...), kind=kLoop, calls=%fused_computation.47 | loop fusion | flops 13762560 | bytes 4206600 | tf_op jit(solution)/shard_map/sub | solution.py:77
  240.5 1.9 multiply_subtract_fusion.39
  242.4 1.5 multiply_subtract_fusion.10
  243.9 7.5 %collective-permute-start.14 = (f32[1,256,4]{2,1,0:T(8,128)S(1)}, f32[1,256,4]{2,1,0:T(8,128)S(1)}, u32[]{:S(2)}, u32[]{:S(2)}) collective-permute-start(f32[1,256,4]{2,1,0:T(8,128)S(1)} %get-tuple-element.110), channel_id=1, source_target_pairs={{8,0},{16,8},{24,16},{32,24},{40,32},{48,40},{56,48},{64,56},{72,6... | collective-permute-start | bytes 12296 | tf_op jit(solution)/shard_map/ppermute | solution.py:24
  251.4 1.9 collective-permute-start.16
  253.4 0.2 maximum_bitcast_fusion.4
  253.6 7.5 %collective-permute-start.17 = (f32[1,256,4]{2,1,0:T(8,128)S(1)}, f32[1,256,4]{2,1,0:T(8,128)S(1)}, u32[]{:S(2)}, u32[]{:S(2)}) collective-permute-start(f32[1,256,4]{2,1,0:T(8,128)S(1)} %get-tuple-element.120), channel_id=1, source_target_pairs={{8,0},{16,8},{24,16},{32,24},{40,32},{48,40},{56,48},{64,56},{72,6... | collective-permute-start | bytes 12296 | tf_op jit(solution)/shard_map/ppermute | solution.py:24
  261.2 1.9 collective-permute-start.19
  263.1 0.2 maximum_bitcast_fusion.5
  263.3 6.9 %multiply_subtract_fusion.21 = (f32[256,256]{1,0:T(8,128)S(1)}, f32[256,256]{1,0:T(8,128)S(1)}, f32[256,256]{1,0:T(8,128)S(1)}, f32[256,256]{1,0:T(8,128)S(1)}, ...) fusion(f32[]{:T(128)} %bitcast.8, ...), kind=kLoop, calls=%fused_computation.43 | loop fusion | flops 13893632 | bytes 4993032 | tf_op jit(solution)/shard_map/sub | solution.py:77
  270.2 1.8 multiply_subtract_fusion.35
  272.0 1.7 multiply_subtract_fusion.7
  273.6 0.9 multiply_subtract_fusion.6
  274.5 7.5 %collective-permute-start.20 = (f32[1,256,4]{2,1,0:T(8,128)S(1)}, f32[1,256,4]{2,1,0:T(8,128)S(1)}, u32[]{:S(2)}, u32[]{:S(2)}) collective-permute-start(f32[1,256,4]{2,1,0:T(8,128)S(1)} %get-tuple-element.108), channel_id=1, source_target_pairs={{8,0},{16,8},{24,16},{32,24},{40,32},{48,40},{56,48},{64,56},{72,6... | collective-permute-start | bytes 12296 | tf_op jit(solution)/shard_map/ppermute | solution.py:24
  282.1 1.9 collective-permute-start.22
  284.0 0.2 maximum_bitcast_fusion.6
  284.3 7.7 %collective-permute-start.23 = (f32[1,256,4]{2,1,0:T(8,128)S(1)}, f32[1,256,4]{2,1,0:T(8,128)S(1)}, u32[]{:S(2)}, u32[]{:S(2)}) collective-permute-start(f32[1,256,4]{2,1,0:T(8,128)S(1)} %get-tuple-element.122), channel_id=1, source_target_pairs={{8,0},{16,8},{24,16},{32,24},{40,32},{48,40},{56,48},{64,56},{72,6... | collective-permute-start | bytes 12296 | tf_op jit(solution)/shard_map/ppermute | solution.py:24
  292.0 0.2 maximum_bitcast_fusion.7
  292.2 6.9 %multiply_subtract_fusion.17 = (f32[256,256]{1,0:T(8,128)S(1)}, f32[256,256]{1,0:T(8,128)S(1)}, f32[256,256]{1,0:T(8,128)S(1)}, f32[256,256]{1,0:T(8,128)S(1)}, ...) fusion(f32[]{:T(128)} %bitcast.12, ...), kind=kLoop, calls=%fused_computation.39 | loop fusion | flops 13893632 | bytes 4993032 | tf_op jit(solution)/shard_map/sub | solution.py:77
  299.1 1.8 multiply_subtract_fusion.31
  300.9 1.7 multiply_subtract_fusion.3
  302.6 0.9 multiply_subtract_fusion.2
  303.6 0.2 maximum_bitcast_fusion.8
  303.8 0.2 maximum_bitcast_fusion.9
  304.0 7.0 %subtract_bitcast_fusion.3 = (f32[1,256,256]{2,1,0:T(8,128)S(1)}, f32[256,256]{1,0:T(8,128)S(1)}, f32[256,256]{1,0:T(8,128)S(1)}, f32[256,256]{1,0:T(8,128)S(1)}...) fusion(f32[]{:T(128)} %bitcast.16, ...), kind=kLoop, calls=%fused_computation.35 | loop fusion | flops 13893632 | bytes 4993032 | tf_op jit(solution)/shard_map/stack | solution.py:104
  311.0 1.9 subtract_bitcast_fusion.5
  312.9 1.8 subtract_bitcast_fusion.2
  314.6 1.0 subtract_bitcast_fusion
  315.6 0.8 maximum_bitcast_fusion.1
  316.4 1.0 maximum_bitcast_fusion
  (38 shorter events, 0.6 us)
Async XLA Ops:
  7.2 153.6 %all-reduce.11.cloned.1.call-start = ((), (), s32[]{:S(2)}) async-start(), calls=%async_computation | async-start | bytes 4194304 | tf_op jit(solution)/shard_map/psum | solution.py:31
  9.5 0.7 copy-start.1
  10.2 0.7 copy-start.3
  160.8 16.0 %collective-permute-start = (f32[1,256,256]{2,1,0:T(8,128)}, f32[1,256,256]{2,1,0:T(8,128)S(1)}, u32[]{:S(2)}, u32[]{:S(2)}) collective-permute-start(f32[1,256,256]{2,1,0:T(8,128)} %get-tuple-element.14), channel_id=1, source_target_pairs={{0,384},{8,392},{16,400},{24,408},{32,416},{40,424},{48,432},{56,4... | collective-permute-start | bytes 786440 | tf_op jit(solution)/shard_map/ppermute | solution.py:12
  162.7 0.7 copy-start.2
  163.5 1.9 copy-start
  163.5 15.5 %collective-permute-start.3 = (f32[1,256,256]{2,1,0:T(8,128)}, f32[1,256,256]{2,1,0:T(8,128)S(1)}, u32[]{:S(2)}, u32[]{:S(2)}) collective-permute-start(f32[1,256,256]{2,1,0:T(8,128)} %get-tuple-element.15), channel_id=1, source_target_pairs={{0,384},{8,392},{16,400},{24,408},{32,416},{40,424},{48,432},{56,4... | collective-permute-start | bytes 786440 | tf_op jit(solution)/shard_map/ppermute | solution.py:12
  166.1 17.2 %collective-permute-start.6 = (f32[1,256,256]{2,1,0:T(8,128)}, f32[1,256,256]{2,1,0:T(8,128)S(1)}, u32[]{:S(2)}, u32[]{:S(2)}) collective-permute-start(f32[1,256,256]{2,1,0:T(8,128)} %get-tuple-element.16), channel_id=1, source_target_pairs={{0,384},{8,392},{16,400},{24,408},{32,416},{40,424},{48,432},{56,4... | collective-permute-start | bytes 786440 | tf_op jit(solution)/shard_map/ppermute | solution.py:12
  168.0 20.9 %collective-permute-start.9 = (f32[1,256,256]{2,1,0:T(8,128)}, f32[1,256,256]{2,1,0:T(8,128)S(1)}, u32[]{:S(2)}, u32[]{:S(2)}) collective-permute-start(f32[1,256,256]{2,1,0:T(8,128)} %get-tuple-element.17), channel_id=1, source_target_pairs={{0,384},{8,392},{16,400},{24,408},{32,416},{40,424},{48,432},{56,4... | collective-permute-start | bytes 786440 | tf_op jit(solution)/shard_map/ppermute | solution.py:12
  174.8 19.7 %collective-permute-start.12 = (f32[1,256,256]{2,1,0:T(8,128)}, f32[1,256,256]{2,1,0:T(8,128)S(1)}, u32[]{:S(2)}, u32[]{:S(2)}) collective-permute-start(f32[1,256,256]{2,1,0:T(8,128)} %get-tuple-element.18), channel_id=1, source_target_pairs={{0,384},{8,392},{16,400},{24,408},{32,416},{40,424},{48,432},{56,4... | collective-permute-start | bytes 786440 | tf_op jit(solution)/shard_map/ppermute | solution.py:12
  176.8 2.2 copy-start.5
  176.8 24.7 %collective-permute-start.15 = (f32[1,256,256]{2,1,0:T(8,128)}, f32[1,256,256]{2,1,0:T(8,128)S(1)}, u32[]{:S(2)}, u32[]{:S(2)}) collective-permute-start(f32[1,256,256]{2,1,0:T(8,128)} %get-tuple-element.19), channel_id=1, source_target_pairs={{0,384},{8,392},{16,400},{24,408},{32,416},{40,424},{48,432},{56,4... | collective-permute-start | bytes 786440 | tf_op jit(solution)/shard_map/ppermute | solution.py:12
  179.0 4.3 %copy-start.4 = (f32[1,256,256]{2,1,0:T(8,128)S(1)}, f32[1,256,256]{2,1,0:T(8,128)}, u32[]{:S(2)}) copy-start(f32[1,256,256]{2,1,0:T(8,128)} %get-tuple-element.21) | copy-start | bytes 786436
  179.0 29.0 %collective-permute-start.18 = (f32[1,256,256]{2,1,0:T(8,128)S(1)}, f32[1,256,256]{2,1,0:T(8,128)S(1)}, u32[]{:S(2)}, u32[]{:S(2)}) collective-permute-start(f32[1,256,256]{2,1,0:T(8,128)S(1)} %copy-done.5), channel_id=1, source_target_pairs={{0,384},{8,392},{16,400},{24,408},{32,416},{40,424},{48,432},{56,4... | collective-permute-start | bytes 786440 | tf_op jit(solution)/shard_map/ppermute | solution.py:12
  183.3 28.9 %collective-permute-start.21 = (f32[1,256,256]{2,1,0:T(8,128)S(1)}, f32[1,256,256]{2,1,0:T(8,128)S(1)}, u32[]{:S(2)}, u32[]{:S(2)}) collective-permute-start(f32[1,256,256]{2,1,0:T(8,128)S(1)} %copy-done.4), channel_id=1, source_target_pairs={{0,384},{8,392},{16,400},{24,408},{32,416},{40,424},{48,432},{56,4... | collective-permute-start | bytes 786440 | tf_op jit(solution)/shard_map/ppermute | solution.py:12
  188.9 25.3 %collective-permute-start.1 = (f32[1,256,4]{2,1,0:T(8,128)S(1)}, f32[1,256,4]{2,1,0:T(8,128)S(1)}, u32[]{:S(2)}, u32[]{:S(2)}) collective-permute-start(f32[1,256,4]{2,1,0:T(8,128)S(1)} %get-tuple-element.113), channel_id=1, source_target_pairs={{0,8},{8,16},{16,24},{24,32},{32,40},{40,48},{48,56},{56,64},{64,7... | collective-permute-start | bytes 12296 | tf_op jit(solution)/shard_map/ppermute | solution.py:21
  194.5 27.3 %collective-permute-start.2 = (f32[1,256,4]{2,1,0:T(8,128)S(1)}, f32[1,256,4]{2,1,0:T(8,128)S(1)}, u32[]{:S(2)}, u32[]{:S(2)}) collective-permute-start(f32[1,256,4]{2,1,0:T(8,128)S(1)} %get-tuple-element.114), channel_id=1, source_target_pairs={{8,0},{16,8},{24,16},{32,24},{40,32},{48,40},{56,48},{64,56},{72,6... | collective-permute-start | bytes 12296 | tf_op jit(solution)/shard_map/ppermute | solution.py:24
  201.5 22.4 %collective-permute-start.4 = (f32[1,256,4]{2,1,0:T(8,128)S(1)}, f32[1,256,4]{2,1,0:T(8,128)S(1)}, u32[]{:S(2)}, u32[]{:S(2)}) collective-permute-start(f32[1,256,4]{2,1,0:T(8,128)S(1)} %get-tuple-element.115), channel_id=1, source_target_pairs={{0,8},{8,16},{16,24},{24,32},{32,40},{40,48},{48,56},{56,64},{64,7... | collective-permute-start | bytes 12296 | tf_op jit(solution)/shard_map/ppermute | solution.py:21
  208.0 23.5 %collective-permute-start.5 = (f32[1,256,4]{2,1,0:T(8,128)S(1)}, f32[1,256,4]{2,1,0:T(8,128)S(1)}, u32[]{:S(2)}, u32[]{:S(2)}) collective-permute-start(f32[1,256,4]{2,1,0:T(8,128)S(1)} %get-tuple-element.116), channel_id=1, source_target_pairs={{8,0},{16,8},{24,16},{32,24},{40,32},{48,40},{56,48},{64,56},{72,6... | collective-permute-start | bytes 12296 | tf_op jit(solution)/shard_map/ppermute | solution.py:24
  212.2 31.7 %collective-permute-start.7 = (f32[1,256,4]{2,1,0:T(8,128)S(1)}, f32[1,256,4]{2,1,0:T(8,128)S(1)}, u32[]{:S(2)}, u32[]{:S(2)}) collective-permute-start(f32[1,256,4]{2,1,0:T(8,128)S(1)} %get-tuple-element.111), channel_id=1, source_target_pairs={{0,8},{8,16},{16,24},{24,32},{32,40},{40,48},{48,56},{56,64},{64,7... | collective-permute-start | bytes 12296 | tf_op jit(solution)/shard_map/ppermute | solution.py:21
  214.2 37.2 %collective-permute-start.8 = (f32[1,256,4]{2,1,0:T(8,128)S(1)}, f32[1,256,4]{2,1,0:T(8,128)S(1)}, u32[]{:S(2)}, u32[]{:S(2)}) collective-permute-start(f32[1,256,4]{2,1,0:T(8,128)S(1)} %get-tuple-element.112), channel_id=1, source_target_pairs={{8,0},{16,8},{24,16},{32,24},{40,32},{48,40},{56,48},{64,56},{72,6... | collective-permute-start | bytes 12296 | tf_op jit(solution)/shard_map/ppermute | solution.py:24
  221.8 31.8 %collective-permute-start.10 = (f32[1,256,4]{2,1,0:T(8,128)S(1)}, f32[1,256,4]{2,1,0:T(8,128)S(1)}, u32[]{:S(2)}, u32[]{:S(2)}) collective-permute-start(f32[1,256,4]{2,1,0:T(8,128)S(1)} %get-tuple-element.117), channel_id=1, source_target_pairs={{0,8},{8,16},{16,24},{24,32},{32,40},{40,48},{48,56},{56,64},{64,7... | collective-permute-start | bytes 12296 | tf_op jit(solution)/shard_map/ppermute | solution.py:21
  224.0 37.2 %collective-permute-start.11 = (f32[1,256,4]{2,1,0:T(8,128)S(1)}, f32[1,256,4]{2,1,0:T(8,128)S(1)}, u32[]{:S(2)}, u32[]{:S(2)}) collective-permute-start(f32[1,256,4]{2,1,0:T(8,128)S(1)} %get-tuple-element.118), channel_id=1, source_target_pairs={{8,0},{16,8},{24,16},{32,24},{40,32},{48,40},{56,48},{64,56},{72,6... | collective-permute-start | bytes 12296 | tf_op jit(solution)/shard_map/ppermute | solution.py:24
  231.5 43.0 %collective-permute-start.13 = (f32[1,256,4]{2,1,0:T(8,128)S(1)}, f32[1,256,4]{2,1,0:T(8,128)S(1)}, u32[]{:S(2)}, u32[]{:S(2)}) collective-permute-start(f32[1,256,4]{2,1,0:T(8,128)S(1)} %get-tuple-element.109), channel_id=1, source_target_pairs={{0,8},{8,16},{16,24},{24,32},{32,40},{40,48},{48,56},{56,64},{64,7... | collective-permute-start | bytes 12296 | tf_op jit(solution)/shard_map/ppermute | solution.py:21
  243.9 38.2 %collective-permute-start.14 = (f32[1,256,4]{2,1,0:T(8,128)S(1)}, f32[1,256,4]{2,1,0:T(8,128)S(1)}, u32[]{:S(2)}, u32[]{:S(2)}) collective-permute-start(f32[1,256,4]{2,1,0:T(8,128)S(1)} %get-tuple-element.110), channel_id=1, source_target_pairs={{8,0},{16,8},{24,16},{32,24},{40,32},{48,40},{56,48},{64,56},{72,6... | collective-permute-start | bytes 12296 | tf_op jit(solution)/shard_map/ppermute | solution.py:24
  251.4 32.8 %collective-permute-start.16 = (f32[1,256,4]{2,1,0:T(8,128)S(1)}, f32[1,256,4]{2,1,0:T(8,128)S(1)}, u32[]{:S(2)}, u32[]{:S(2)}) collective-permute-start(f32[1,256,4]{2,1,0:T(8,128)S(1)} %get-tuple-element.119), channel_id=1, source_target_pairs={{0,8},{8,16},{16,24},{24,32},{32,40},{40,48},{48,56},{56,64},{64,7... | collective-permute-start | bytes 12296 | tf_op jit(solution)/shard_map/ppermute | solution.py:21
  253.6 38.4 %collective-permute-start.17 = (f32[1,256,4]{2,1,0:T(8,128)S(1)}, f32[1,256,4]{2,1,0:T(8,128)S(1)}, u32[]{:S(2)}, u32[]{:S(2)}) collective-permute-start(f32[1,256,4]{2,1,0:T(8,128)S(1)} %get-tuple-element.120), channel_id=1, source_target_pairs={{8,0},{16,8},{24,16},{32,24},{40,32},{48,40},{56,48},{64,56},{72,6... | collective-permute-start | bytes 12296 | tf_op jit(solution)/shard_map/ppermute | solution.py:24
  261.2 42.4 %collective-permute-start.19 = (f32[1,256,4]{2,1,0:T(8,128)S(1)}, f32[1,256,4]{2,1,0:T(8,128)S(1)}, u32[]{:S(2)}, u32[]{:S(2)}) collective-permute-start(f32[1,256,4]{2,1,0:T(8,128)S(1)} %get-tuple-element.107), channel_id=1, source_target_pairs={{0,8},{8,16},{16,24},{24,32},{32,40},{40,48},{48,56},{56,64},{64,7... | collective-permute-start | bytes 12296 | tf_op jit(solution)/shard_map/ppermute | solution.py:21
  274.5 29.0 %collective-permute-start.20 = (f32[1,256,4]{2,1,0:T(8,128)S(1)}, f32[1,256,4]{2,1,0:T(8,128)S(1)}, u32[]{:S(2)}, u32[]{:S(2)}) collective-permute-start(f32[1,256,4]{2,1,0:T(8,128)S(1)} %get-tuple-element.108), channel_id=1, source_target_pairs={{8,0},{16,8},{24,16},{32,24},{40,32},{48,40},{56,48},{64,56},{72,6... | collective-permute-start | bytes 12296 | tf_op jit(solution)/shard_map/ppermute | solution.py:24
  282.1 21.7 %collective-permute-start.22 = (f32[1,256,4]{2,1,0:T(8,128)S(1)}, f32[1,256,4]{2,1,0:T(8,128)S(1)}, u32[]{:S(2)}, u32[]{:S(2)}) collective-permute-start(f32[1,256,4]{2,1,0:T(8,128)S(1)} %get-tuple-element.121), channel_id=1, source_target_pairs={{0,8},{8,16},{16,24},{24,32},{32,40},{40,48},{48,56},{56,64},{64,7... | collective-permute-start | bytes 12296 | tf_op jit(solution)/shard_map/ppermute | solution.py:21
  284.3 19.5 %collective-permute-start.23 = (f32[1,256,4]{2,1,0:T(8,128)S(1)}, f32[1,256,4]{2,1,0:T(8,128)S(1)}, u32[]{:S(2)}, u32[]{:S(2)}) collective-permute-start(f32[1,256,4]{2,1,0:T(8,128)S(1)} %get-tuple-element.122), channel_id=1, source_target_pairs={{8,0},{16,8},{24,16},{32,24},{40,32},{48,40},{56,48},{64,56},{72,6... | collective-permute-start | bytes 12296 | tf_op jit(solution)/shard_map/ppermute | solution.py:24
Sparse Core Ops, SparseCore 0:
  12.1 148.6 all-reduce.10
where the time goes:
time: 325 us; the launch traced here: 324 us
  waiting for transfers between devices  165 us (51%)
  starting transfers between devices  91.6 us (28%)
  other arithmetic  50.1 us (15%)
  between operations  14.6 us (4%)
  local copies, waits for them, and re-layouts  3.43 us (1%)
    psum x1, waiting for transfers between devices, from_root(): return lax.psum(jnp.where(mine, shard, jnp.zeros_like(shard)), axis)  150 us
    ppermute x8, starting transfers between devices, extended(): lax.ppermute(lax.slice_in_dim(block, 0, width, axis=dim), axis, backward)  52.5 us
    ppermute x8, starting transfers between devices, shifted(): return lax.ppermute(value, axis, pairs)  23.7 us
    sub x3, other arithmetic, advance(): b_zz = a_zz - gain * (shear_tt * a_zz + shear_tp * a_oz)  20.6 us
    ppermute x8, starting transfers between devices, extended(): lax.ppermute(lax.slice_in_dim(block, block.shape[dim] - width, None, axis...  15.3 us
    ppermute x8, waiting for transfers between devices, shifted(): return lax.ppermute(value, axis, pairs)  14.6 us
    another operation x3, other arithmetic, per_device(): jacobian = jnp.stack(state[2:6])[None]  9.68 us
  transfers between devices with their start and end apart: 25, of which 7 were waited for; matrix products, arithmetic and copies ran while one was open for 11% of the time, Pallas kernels for 0%

commit v1 on v0

v1 whole, which is shorter than its diff:
```python
import jax
import jax.numpy as jnp
from jax import lax
from jax.experimental import pallas as pl
from jax.experimental.pallas import tpu as pltpu
from jax.sharding import PartitionSpec as P

HALO = 4
TAPS = 7
PAD = 16
Z_LO, Z_HI, NX, RING = 4, 2, 4, 16


def z_move(value, ahead, steps=0):
    pairs = []
    for z_lo in range(Z_LO):
        for z_hi in range(Z_HI):
            for ring in range(RING):
                for x in range(NX):
                    z = (z_hi * Z_LO + z_lo + ahead) % (Z_LO * Z_HI)
                    lon = (((z_lo + 1) % Z_LO) * RING + ring + steps) % (Z_LO * RING)
                    source = lon * Z_HI * NX + (z // Z_LO) * NX + x
                    target = (z_lo * RING + ring) * Z_HI * NX + z_hi * NX + x
                    pairs.append((source, target))
    return lax.ppermute(value, ("lon", "plane"), pairs)


def x_move(value, ahead):
    pairs = [
        (z_hi * NX + (x + ahead) % NX, z_hi * NX + x) for z_hi in range(Z_HI) for x in range(NX)
    ]
    return lax.ppermute(value, "plane", pairs)


def load_planes(slot_ref, tiles, ext):
    for ahead, tile in enumerate(tiles):
        slot = slot_ref[ahead]
        width = tile.shape[1]
        for half in range(2):
            rows = slice(half * 128, half * 128 + 128)
            ext[slot, half, PAD : PAD + width, :] = tile[rows, :].T
            ext[slot, half, PAD - HALO : PAD, :] = tile[width : width + HALO, rows]
            ext[slot, half, PAD + width : PAD + width + HALO, :] = tile[
                width + HALO : width + 2 * HALO, rows
            ]


def neighbours(width, taps_ref, ext, diff, both):
    lane = lax.broadcasted_iota(jnp.int32, (8, 128), 1)
    first, last = lane == 0, lane == 127

    def block(j, carry):
        at = pl.multiple_of(j * 8, 8) + PAD - 8
        norths, souths = [], []
        for half in range(2):
            north_of, south_of = [], []
            for slot in range(NX):
                views = [ext[slot, half, pl.ds(at + tap - 3, 8), :] for tap in range(TAPS)]
                north = views[0] * taps_ref[0, half]
                south = views[0] * taps_ref[TAPS, half]
                for tap in range(1, TAPS):
                    north += views[tap] * taps_ref[tap, half]
                    south += views[tap] * taps_ref[TAPS + tap, half]
                north_of.append(pltpu.roll(north, 1, 1))
                south_of.append(pltpu.roll(south, 127, 1))
            norths.append(north_of)
            souths.append(south_of)
        for slot in range(NX):
            n = [
                jnp.where(first, 0.0, norths[0][slot]),
                jnp.where(first, norths[0][slot], norths[1][slot]),
            ]
            s = [
                jnp.where(last, souths[1][slot], souths[0][slot]),
                jnp.where(last, 0.0, souths[1][slot]),
            ]
            for half in range(2):
                diff[slot, half, pl.ds(at, 8), :] = s[half] - n[half]
                both[slot, half, pl.ds(at, 8), :] = s[half] + n[half]
        return carry

    lax.fori_loop(0, width // 8 + 2, block, 0)


def compose(at, half, hi, gain_ref, metric_ref, ext, diff, both):
    half_m, square_m, quarter_m = metric_ref[0, half], metric_ref[1, half], metric_ref[2, half]
    state = None
    for slot in range(NX):
        gain = gain_ref[hi * NX + slot]
        centre = ext[slot, half, pl.ds(at, 8), :]
        east = ext[slot, half, pl.ds(at + 1, 8), :]
        west = ext[slot, half, pl.ds(at - 1, 8), :]
        twice = centre + centre
        alpha_t = (0.5 * gain) * diff[slot, half, pl.ds(at, 8), :]
        alpha_p = (gain * half_m) * (east - west)
        u_tt = gain * (both[slot, half, pl.ds(at, 8), :] - twice)
        u_pp = (gain * square_m) * ((east + west) - twice)
        u_tp = (gain * quarter_m) * (
            diff[slot, half, pl.ds(at + 1, 8), :] - diff[slot, half, pl.ds(at - 1, 8), :]
        )
        if state is None:
            state = (-alpha_t, -alpha_p, 1.0 - u_tt, -u_tp, -u_tp, 1.0 - u_pp)
        else:
            d_t, d_p, a_zz, a_zo, a_oz, a_oo = state
            state = (
                d_t - (alpha_t + (u_tt * d_t + u_tp * d_p)),
                d_p - (alpha_p + (u_tp * d_t + u_pp * d_p)),
                a_zz - (u_tt * a_zz + u_tp * a_oz),
                a_zo - (u_tt * a_zo + u_tp * a_oo),
                a_oz - (u_tp * a_zz + u_pp * a_oz),
                a_oo - (u_tp * a_zo + u_pp * a_oo),
            )
    return state


def first_kernel(slot_ref, gain_ref, taps_ref, metric_ref, t0, t1, t2, t3, out, ext, diff, both):
    width = t0.shape[1]
    load_planes(slot_ref, (t0, t1, t2, t3), ext)
    neighbours(width, taps_ref, ext, diff, both)
    hi = slot_ref[NX]

    def block(j, carry):
        at = pl.multiple_of(j * 8, 8)
        for half in range(2):
            state = compose(at + PAD, half, hi, gain_ref, metric_ref, ext, diff, both)
            for k in range(6):
                out[k, half, pl.ds(at, 8), :] = state[k]
        return carry

    lax.fori_loop(0, width // 8, block, 0)


def second_kernel(
    slot_ref, gain_ref, taps_ref, metric_ref, t0, t1, t2, t3, other, disp, jac, ext, diff, both, done
):
    width = t0.shape[1]
    load_planes(slot_ref, (t0, t1, t2, t3), ext)
    neighbours(width, taps_ref, ext, diff, both)
    hi = 1 - slot_ref[NX]
    other_first = hi == 1

    def block(j, carry):
        at = pl.multiple_of(j * 8, 8)
        for half in range(2):
            here = compose(at + PAD, half, hi, gain_ref, metric_ref, ext, diff, both)
            there = [other[k, half, pl.ds(at, 8), :] for k in range(6)]
            d_t, d_p, a_zz, a_zo, a_oz, a_oo = [
                jnp.where(other_first, a, b) for a, b in zip(there, here)
            ]
            e_t, e_p, b_zz, b_zo, b_oz, b_oo = [
                jnp.where(other_first, b, a) for a, b in zip(there, here)
            ]
            state = (
                e_t + (b_zz * d_t + b_zo * d_p),
                e_p + (b_oz * d_t + b_oo * d_p),
                b_zz * a_zz + b_zo * a_oz,
                b_zz * a_zo + b_zo * a_oo,
                b_oz * a_zz + b_oo * a_oz,
                b_oz * a_zo + b_oo * a_oo,
            )
            for k in range(6):
                done[k, half, pl.ds(at, 8), :] = state[k]
        return carry

    lax.fori_loop(0, width // 8, block, 0)
    for k in range(6):
        for half in range(2):
            rows = slice(half * 128, half * 128 + 128)
            turned = done[k, half].T
            if k < 2:
                disp[k, rows, :] = turned
            else:
                jac[k - 2, rows, :] = turned


def smem():
    return pl.BlockSpec(memory_space=pltpu.SMEM)


def vmem():
    return pl.BlockSpec(memory_space=pltpu.VMEM)


def planes_scratch(width):
    return [pltpu.VMEM((NX, 2, width + 2 * PAD, 128), jnp.float32)] * 3


def cost(rows, width):
    return pl.CostEstimate(
        flops=260 * NX * rows * width, bytes_accessed=40 * rows * width, transcendentals=0
    )


def prepare_kernel(tile_ref, shift_ref, weight_ref, scale_ref, low, high, taps, metric):
    rows, width = tile_ref.shape
    for half in range(2):
        lanes = slice(half * 128, half * 128 + 128)
        low[:, lanes] = tile_ref[lanes, width - 128 :].T[128 - HALO :]
        high[:, lanes] = tile_ref[lanes, :128].T[:HALO]
    for side, turn in ((0, rows - 1), (1, 1)):
        shift = jnp.broadcast_to(shift_ref[side : side + 1, :], (8, rows))
        frac = jnp.broadcast_to(weight_ref[side : side + 1, :].astype(jnp.float32) / 16.0, (8, rows))
        shift, frac = pltpu.roll(shift, turn, 1), pltpu.roll(frac, turn, 1)
        for tap in range(TAPS):
            value = jnp.where(shift == tap - 3, 1.0 - frac, 0.0)
            value += jnp.where(shift == tap - 4, frac, 0.0)
            for half in range(2):
                taps[side * TAPS + tap, half] = value[:, half * 128 : half * 128 + 128]
    scale = jnp.broadcast_to(scale_ref[...], (8, rows))
    for k, value in enumerate((0.5 * scale, scale * scale, 0.25 * scale)):
        for half in range(2):
            metric[k, half] = value[:, half * 128 : half * 128 + 128]


def prepare(tile, cycle_shift, cycle_weight, cycle_scale):
    rows = tile.shape[0]
    return pl.pallas_call(
        prepare_kernel,
        out_shape=(
            jax.ShapeDtypeStruct((HALO, rows), jnp.float32),
            jax.ShapeDtypeStruct((HALO, rows), jnp.float32),
            jax.ShapeDtypeStruct((2 * TAPS, 2, 8, rows // 2), jnp.float32),
            jax.ShapeDtypeStruct((3, 2, 8, rows // 2), jnp.float32),
        ),
        in_specs=[vmem()] * 4,
        out_specs=(vmem(),) * 4,
        cost_estimate=pl.CostEstimate(flops=1 << 16, bytes_accessed=1 << 20, transcendentals=0),
        name="prepare",
    )(tile, cycle_shift, cycle_weight, cycle_scale[None])


def per_device(potential, lens_weight, cycle_shift, cycle_weight, cycle_scale):
    tile = potential[0]
    rows, width = tile.shape
    gains = lens_weight[0]
    lon, plane = lax.axis_index("lon"), lax.axis_index("plane")
    x = plane % NX
    near_hi = (((plane // NX) * Z_LO + lon // RING + 1) // Z_LO) % Z_HI
    order = jnp.arange(2 * NX, dtype=jnp.int32)
    scalars = jnp.where(order < NX, (x + order) % NX, near_hi).astype(jnp.int32)

    near = z_move(tile, 1)
    far = z_move(tile, 1 + Z_LO)
    low, high, taps, metric = prepare(tile, cycle_shift, cycle_weight, cycle_scale)

    def group(own, low, high, ahead):
        whole = jnp.concatenate([own, z_move(low, ahead, -1), z_move(high, ahead, 1)])
        return (whole, x_move(whole, 1), x_move(whole, 2), x_move(whole, 3))

    near_tiles = group(near, low, high, 1)
    low, high, _ = lax.optimization_barrier((low, high, near_tiles[0]))
    far_tiles = group(far, low, high, 1 + Z_LO)

    state = pl.pallas_call(
        first_kernel,
        out_shape=jax.ShapeDtypeStruct((6, 2, width, rows // 2), jnp.float32),
        in_specs=[smem(), smem()] + [vmem()] * 6,
        out_specs=vmem(),
        scratch_shapes=planes_scratch(width),
        cost_estimate=cost(rows, width),
        compiler_params=pltpu.CompilerParams(vmem_limit_bytes=24 << 20),
        name="near_planes",
    )(scalars, gains, taps, metric, *near_tiles)
    displacement, jacobian = pl.pallas_call(
        second_kernel,
        out_shape=(
            jax.ShapeDtypeStruct((2, rows, width), jnp.float32),
            jax.ShapeDtypeStruct((4, rows, width), jnp.float32),
        ),
        in_specs=[smem(), smem()] + [vmem()] * 7,
        out_specs=(vmem(), vmem()),
        scratch_shapes=planes_scratch(width)
        + [pltpu.VMEM((6, 2, width, rows // 2), jnp.float32)],
        cost_estimate=cost(rows, width),
        compiler_params=pltpu.CompilerParams(vmem_limit_bytes=24 << 20),
        name="far_planes",
    )(scalars, gains, taps, metric, *far_tiles, state)
    return displacement[None], jacobian[None]


def solution(mesh):
    in_specs = (P("plane", None, "lon"), P("plane", None), P(), P(), P())
    out_specs = (P("plane", None, None, "lon"), P("plane", None, None, "lon"))
    return jax.shard_map(
        per_device, mesh=mesh, in_specs=in_specs, out_specs=out_specs, check_vma=False
    )
```

time: 325 us -> 78.8 us (0.24)
  waiting for transfers between devices: 165 us -> 6.68 us
  other arithmetic: 50.1 us -> 0.05 us
  starting transfers between devices: 91.6 us -> 52.4 us
  Pallas kernels: 0 us -> 16 us
  between operations: 14.6 us -> 0.89 us
    psum x1 -> x0, waiting for transfers between devices: 150 us -> none  [from_root(): return lax.psum(jnp.where(mine, shard, jnp.zeros_like(shard)), axis)]
    ppermute x24 -> x12, starting transfers between devices: 91.5 us -> 52.4 us  [the longest x6 32.6 us: z_move(): return lax.ppermute(value, ('lon', 'plane'), pairs)]
    sub x12 -> x0, other arithmetic: 32.7 us -> none  [the longest x3 20.6 us: advance(): b_zz = a_zz - gain * (shear_tt * a_zz + shear_tp * a_oz)]
    pallas_call x0 -> x3, Pallas kernels: none -> 16 us  [the longest x1 7.91 us: per_device(): pl.pallas_call(second_kernel, out_shape=(jax.ShapeDtypeStruct((2, rows, w...]
    another operation x4 -> x0, other arithmetic: 11.5 us -> none  [the longest x3 9.68 us: per_device(): jacobian = jnp.stack(state[2:6])[None]]
    ppermute x24 -> x12, waiting for transfers between devices: 14.6 us -> 6.68 us  [the longest x6 4.38 us: x_move(): return lax.ppermute(value, 'plane', pairs)]
  transfers between devices with their start and end apart: 25 -> 12, of which waited for: 7 -> 3; matrix products, arithmetic and copies ran while one was open for 11% -> 0% of each run, Pallas kernels for 0% -> 10%
where the time goes in v1:
time: 78.8 us; the launch traced here: 78.3 us
  starting transfers between devices  52.4 us (66%)
  Pallas kernels  16 us (20%)
  waiting for transfers between devices  6.68 us (8%)
  local copies, waits for them, and re-layouts  2.29 us (3%)
  between operations  0.89 us (1%)
    ppermute x6, starting transfers between devices, z_move(): return lax.ppermute(value, ('lon', 'plane'), pairs)  32.6 us
    ppermute x6, starting transfers between devices, x_move(): return lax.ppermute(value, 'plane', pairs)  19.9 us
    pallas_call x1, Pallas kernels, per_device(): pl.pallas_call(second_kernel, out_shape=(jax.ShapeDtypeStruct((2, rows, w...  7.91 us
    pallas_call x1, Pallas kernels, per_device(): pl.pallas_call(first_kernel, out_shape=jax.ShapeDtypeStruct((6, 2, width,...  6.27 us
    ppermute x6, waiting for transfers between devices, x_move(): return lax.ppermute(value, 'plane', pairs)  4.38 us
    ppermute x6, waiting for transfers between devices, z_move(): return lax.ppermute(value, ('lon', 'plane'), pairs)  2.3 us
    unnamed x6, local copies, waits for them, and re-layouts  2.29 us
    pallas_call x1, Pallas kernels, prepare(): pl.pallas_call(prepare_kernel, out_shape=(jax.ShapeDtypeStruct((HALO, row...  1.8 us
  transfers between devices with their start and end apart: 12, of which 3 were waited for; matrix products, arithmetic and copies ran while one was open for 0% of the time, Pallas kernels for 10%

profile of v1, /device:TPU:6, one launch (start us, length us, event | category | flops | bytes accessed | tf_op | source)
XLA Modules:
  0.0 78.3 jit_solution(6251088470633425644)
XLA Ops:
  0.6 10.9 %collective-permute-start.1 = (f32[256,256]{1,0:T(8,128)}, f32[256,256]{1,0:T(8,128)S(1)}, u32[]{:S(2)}, u32[]{:S(2)}) collective-permute-start(f32[256,256]{1,0:T(8,128)} %bitcast.7), channel_id=1, source_target_pairs={{128,0},{129,1},{130,2},{131,3},{136,8},{137,9},{138,10},{139,11},... | collective-permute-start | bytes 786440 | tf_op jit(solution)/shard_map/ppermute | solution.py:25
  11.6 1.8 %prepare.1 = (f32[4,256]{1,0:T(4,128)}, f32[4,256]{1,0:T(4,128)}, f32[14,2,8,128]{3,2,1,0:T(8,128)}, f32[3,2,8,128]{3,2,1,0:T(8,128)}) custom-call(f32[256,256]{1,0:T(8,128)} %bitcast.8, s32[2,256]{1,0:T(2,128)} %shift_ref.1, s32[2,256]{1,0:T(2,128)} %weight_ref.1, f32[1,256]{1,0:T(1,128)} %bitcast.10), custom_call_target="tpu_custom_call" | custom-call | flops 65536 | bytes 1048576 | tf_op jit(solution)/shard_map/prepare/pallas_call | solution.py:217
  13.4 1.9 %collective-permute-start.2 = (f32[4,256]{1,0:T(4,128)}, f32[4,256]{1,0:T(4,128)S(1)}, u32[]{:S(2)}, u32[]{:S(2)}) collective-permute-start(f32[4,256]{1,0:T(4,128)} %get-tuple-element.14), channel_id=1, source_target_pairs={{120,0},{121,1},{122,2},{123,3},{128,8},{129,9},{130,10},{131,11},... | collective-permute-start | bytes 12296 | tf_op jit(solution)/shard_map/ppermute | solution.py:25
  15.3 1.9 %collective-permute-start.3 = (f32[4,256]{1,0:T(4,128)}, f32[4,256]{1,0:T(4,128)S(1)}, u32[]{:S(2)}, u32[]{:S(2)}) collective-permute-start(f32[4,256]{1,0:T(4,128)} %get-tuple-element.15), channel_id=1, source_target_pairs={{136,0},{137,1},{138,2},{139,3},{144,8},{145,9},{146,10},{147,11},... | collective-permute-start | bytes 12296 | tf_op jit(solution)/shard_map/ppermute | solution.py:25
  17.2 1.9 %collective-permute-start = (f32[256,256]{1,0:T(8,128)}, f32[256,256]{1,0:T(8,128)S(1)}, u32[]{:S(2)}, u32[]{:S(2)}) collective-permute-start(f32[256,256]{1,0:T(8,128)} %bitcast.9), channel_id=1, source_target_pairs={{132,0},{133,1},{134,2},{135,3},{140,8},{141,9},{142,10},{143,11},... | collective-permute-start | bytes 786440 | tf_op jit(solution)/shard_map/ppermute | solution.py:25
  19.2 0.6 collective-permute-done.2
  19.7 1.7 %collective-permute-done.3 = f32[4,256]{1,0:T(4,128)S(1)} collective-permute-done((f32[4,256]{1,0:T(4,128)}, f32[4,256]{1,0:T(4,128)S(1)}, u32[]{:S(2)}, u32[]{:S(2)}) %collective-permute-start.3) | collective-permute-done | bytes 4128 | tf_op jit(solution)/shard_map/ppermute | solution.py:25
  21.4 0.0 collective-permute-done.1
  21.5 3.2 %collective-permute-start.11 = (f32[264,256]{1,0:T(8,128)S(1)}, f32[264,256]{1,0:T(8,128)S(1)}, u32[]{:S(2)}, u32[]{:S(2)}) collective-permute-start(f32[264,256]{1,0:T(8,128)S(1)} %pad_maximum_fusion.t0), channel_id=1, source_target_pairs={{3,0},{0,1},{1,2},{2,3},{7,4},{4,5},{5,6},{6,7},{11,8},{8,9},{9,10... | collective-permute-start | bytes 811016 | tf_op jit(solution)/shard_map/ppermute | solution.py:32
  24.7 2.4 %collective-permute-start.4 = (f32[4,256]{1,0:T(4,128)}, f32[4,256]{1,0:T(4,128)S(1)}, u32[]{:S(2)}, u32[]{:S(2)}) collective-permute-start(f32[4,256]{1,0:T(4,128)} %get-tuple-element.14), channel_id=1, source_target_pairs={{124,0},{125,1},{126,2},{127,3},{132,8},{133,9},{134,10},{135,11},... | collective-permute-start | bytes 12296 | tf_op jit(solution)/shard_map/ppermute | solution.py:25
  27.1 13.4 %collective-permute-start.5 = (f32[4,256]{1,0:T(4,128)}, f32[4,256]{1,0:T(4,128)S(1)}, u32[]{:S(2)}, u32[]{:S(2)}) collective-permute-start(f32[4,256]{1,0:T(4,128)} %get-tuple-element.15), channel_id=1, source_target_pairs={{140,0},{141,1},{142,2},{143,3},{148,8},{149,9},{150,10},{151,11},... | collective-permute-start | bytes 12296 | tf_op jit(solution)/shard_map/ppermute | solution.py:25
  40.6 4.3 %collective-permute-start.10 = (f32[264,256]{1,0:T(8,128)S(1)}, f32[264,256]{1,0:T(8,128)S(1)}, u32[]{:S(2)}, u32[]{:S(2)}) collective-permute-start(f32[264,256]{1,0:T(8,128)S(1)} %pad_maximum_fusion.t0), channel_id=1, source_target_pairs={{2,0},{3,1},{0,2},{1,3},{6,4},{7,5},{4,6},{5,7},{10,8},{11,9},{8,1... | collective-permute-start | bytes 811016 | tf_op jit(solution)/shard_map/ppermute | solution.py:32
  44.9 0.0 collective-permute-done
  44.9 1.9 %collective-permute-start.9 = (f32[264,256]{1,0:T(8,128)S(1)}, f32[264,256]{1,0:T(8,128)S(1)}, u32[]{:S(2)}, u32[]{:S(2)}) collective-permute-start(f32[264,256]{1,0:T(8,128)S(1)} %pad_maximum_fusion.t0), channel_id=1, source_target_pairs={{1,0},{2,1},{3,2},{0,3},{5,4},{6,5},{7,6},{4,7},{9,8},{10,9},{11,1... | collective-permute-start | bytes 811016 | tf_op jit(solution)/shard_map/ppermute | solution.py:32
  46.9 0.0 collective-permute-done.4
  46.9 0.0 collective-permute-done.5
  46.9 5.1 %collective-permute-start.8 = (f32[264,256]{1,0:T(8,128)S(1)}, f32[264,256]{1,0:T(8,128)S(1)}, u32[]{:S(2)}, u32[]{:S(2)}) collective-permute-start(f32[264,256]{1,0:T(8,128)S(1)} %pad_maximum_fusion.1.t0), channel_id=1, source_target_pairs={{3,0},{0,1},{1,2},{2,3},{7,4},{4,5},{5,6},{6,7},{11,8},{8,9},{9,10... | collective-permute-start | bytes 811016 | tf_op jit(solution)/shard_map/ppermute | solution.py:32
  52.1 1.9 %collective-permute-start.7 = (f32[264,256]{1,0:T(8,128)S(1)}, f32[264,256]{1,0:T(8,128)S(1)}, u32[]{:S(2)}, u32[]{:S(2)}) collective-permute-start(f32[264,256]{1,0:T(8,128)S(1)} %pad_maximum_fusion.1.t0), channel_id=1, source_target_pairs={{2,0},{3,1},{0,2},{1,3},{6,4},{7,5},{4,6},{5,7},{10,8},{11,9},{8,1... | collective-permute-start | bytes 811016 | tf_op jit(solution)/shard_map/ppermute | solution.py:32
  54.0 0.0 collective-permute-done.11.t3
  54.0 3.3 %collective-permute-start.6 = (f32[264,256]{1,0:T(8,128)S(1)}, f32[264,256]{1,0:T(8,128)S(1)}, u32[]{:S(2)}, u32[]{:S(2)}) collective-permute-start(f32[264,256]{1,0:T(8,128)S(1)} %pad_maximum_fusion.1.t0), channel_id=1, source_target_pairs={{1,0},{2,1},{3,2},{0,3},{5,4},{6,5},{7,6},{4,7},{9,8},{10,9},{11,1... | collective-permute-start | bytes 811016 | tf_op jit(solution)/shard_map/ppermute | solution.py:32
  57.4 0.0 collective-permute-done.10.t2
  57.4 4.4 %collective-permute-done.9.t1 = f32[264,256]{1,0:T(8,128)S(1)} collective-permute-done((f32[264,256]{1,0:T(8,128)S(1)}, f32[264,256]{1,0:T(8,128)S(1)}, u32[]{:S(2)}, u32[]{:S(2)}) %collective-permute-start.9) | collective-permute-done | bytes 270368 | tf_op jit(solution)/shard_map/ppermute | solution.py:32
  61.8 0.0 copy-start
  61.8 0.9 %copy-done = f32[14,2,8,128]{3,2,1,0:T(8,128)S(1)} copy-done((f32[14,2,8,128]{3,2,1,0:T(8,128)S(1)}, f32[14,2,8,128]{3,2,1,0:T(8,128)}, u32[]{:S(2)}) %copy-start) | copy-done | bytes 114712
  62.7 0.0 copy-start.1
  62.7 0.7 copy-done.1
  63.4 0.0 copy-start.2
  63.4 0.7 copy-done.2
  64.1 6.3 %near_planes.1.other = f32[6,2,256,128]{3,2,1,0:T(8,128)S(1)} custom-call(s32[8]{0:T(128)S(1)} %compare_select_fusion.2.slot_ref, f32[8]{0:T(128)S(1)} %bitcast.5, f32[14,2,8,128]{3,2,1,0:T(8,128)S(1)} %copy-done, f32[3,2,8,128]{3,2,1,0:T(8,128)S(1)} %copy-done.1, f32[264,256]{1,0:T(8,128)S(1)} %pad_maximum_fusion.t0, ...), custom_call_target="tpu_custom_call" | custom-call | flops 68157440 | bytes 2621440 | tf_op jit(solution)/shard_map/near_planes/pallas_call | solution.py:254
  70.4 0.0 collective-permute-done.8.t3
  70.4 0.0 collective-permute-done.7.t2
  70.4 0.0 collective-permute-done.6.t1
  70.4 7.9 %far_planes.1 = (f32[2,256,256]{2,1,0:T(8,128)}, f32[4,256,256]{2,1,0:T(8,128)}) custom-call(s32[8]{0:T(128)S(1)} %compare_select_fusion.2.slot_ref, f32[8]{0:T(128)S(1)} %bitcast.6, f32[14,2,8,128]{3,2,1,0:T(8,128)S(1)} %copy-done, f32[3,2,8,128]{3,2,1,0:T(8,128)S(1)} %copy-done.1, f32[264,256]{1,0:T(8,128)S(1)} %pad_maximum_fusion.1.t0, ...), custom_call_target="tpu_custom_call" | custom-call | flops 68157440 | bytes 2621440 | tf_op jit(solution)/shard_map/far_planes/pallas_call | solution.py:264
  (3 shorter events, 0.1 us)
Async XLA Ops:
  0.6 20.8 %collective-permute-start.1 = (f32[256,256]{1,0:T(8,128)}, f32[256,256]{1,0:T(8,128)S(1)}, u32[]{:S(2)}, u32[]{:S(2)}) collective-permute-start(f32[256,256]{1,0:T(8,128)} %bitcast.7), channel_id=1, source_target_pairs={{128,0},{129,1},{130,2},{131,3},{136,8},{137,9},{138,10},{139,11},... | collective-permute-start | bytes 786440 | tf_op jit(solution)/shard_map/ppermute | solution.py:25
  13.4 6.3 %collective-permute-start.2 = (f32[4,256]{1,0:T(4,128)}, f32[4,256]{1,0:T(4,128)S(1)}, u32[]{:S(2)}, u32[]{:S(2)}) collective-permute-start(f32[4,256]{1,0:T(4,128)} %get-tuple-element.14), channel_id=1, source_target_pairs={{120,0},{121,1},{122,2},{123,3},{128,8},{129,9},{130,10},{131,11},... | collective-permute-start | bytes 12296 | tf_op jit(solution)/shard_map/ppermute | solution.py:25
  15.3 6.1 %collective-permute-start.3 = (f32[4,256]{1,0:T(4,128)}, f32[4,256]{1,0:T(4,128)S(1)}, u32[]{:S(2)}, u32[]{:S(2)}) collective-permute-start(f32[4,256]{1,0:T(4,128)} %get-tuple-element.15), channel_id=1, source_target_pairs={{136,0},{137,1},{138,2},{139,3},{144,8},{145,9},{146,10},{147,11},... | collective-permute-start | bytes 12296 | tf_op jit(solution)/shard_map/ppermute | solution.py:25
  17.2 27.7 %collective-permute-start = (f32[256,256]{1,0:T(8,128)}, f32[256,256]{1,0:T(8,128)S(1)}, u32[]{:S(2)}, u32[]{:S(2)}) collective-permute-start(f32[256,256]{1,0:T(8,128)} %bitcast.9), channel_id=1, source_target_pairs={{132,0},{133,1},{134,2},{135,3},{140,8},{141,9},{142,10},{143,11},... | collective-permute-start | bytes 786440 | tf_op jit(solution)/shard_map/ppermute | solution.py:25
  21.5 32.5 %collective-permute-start.11 = (f32[264,256]{1,0:T(8,128)S(1)}, f32[264,256]{1,0:T(8,128)S(1)}, u32[]{:S(2)}, u32[]{:S(2)}) collective-permute-start(f32[264,256]{1,0:T(8,128)S(1)} %pad_maximum_fusion.t0), channel_id=1, source_target_pairs={{3,0},{0,1},{1,2},{2,3},{7,4},{4,5},{5,6},{6,7},{11,8},{8,9},{9,10... | collective-permute-start | bytes 811016 | tf_op jit(solution)/shard_map/ppermute | solution.py:32
  24.7 22.2 %collective-permute-start.4 = (f32[4,256]{1,0:T(4,128)}, f32[4,256]{1,0:T(4,128)S(1)}, u32[]{:S(2)}, u32[]{:S(2)}) collective-permute-start(f32[4,256]{1,0:T(4,128)} %get-tuple-element.14), channel_id=1, source_target_pairs={{124,0},{125,1},{126,2},{127,3},{132,8},{133,9},{134,10},{135,11},... | collective-permute-start | bytes 12296 | tf_op jit(solution)/shard_map/ppermute | solution.py:25
  27.1 19.7 %collective-permute-start.5 = (f32[4,256]{1,0:T(4,128)}, f32[4,256]{1,0:T(4,128)S(1)}, u32[]{:S(2)}, u32[]{:S(2)}) collective-permute-start(f32[4,256]{1,0:T(4,128)} %get-tuple-element.15), channel_id=1, source_target_pairs={{140,0},{141,1},{142,2},{143,3},{148,8},{149,9},{150,10},{151,11},... | collective-permute-start | bytes 12296 | tf_op jit(solution)/shard_map/ppermute | solution.py:25
  40.6 16.8 %collective-permute-start.10 = (f32[264,256]{1,0:T(8,128)S(1)}, f32[264,256]{1,0:T(8,128)S(1)}, u32[]{:S(2)}, u32[]{:S(2)}) collective-permute-start(f32[264,256]{1,0:T(8,128)S(1)} %pad_maximum_fusion.t0), channel_id=1, source_target_pairs={{2,0},{3,1},{0,2},{1,3},{6,4},{7,5},{4,6},{5,7},{10,8},{11,9},{8,1... | collective-permute-start | bytes 811016 | tf_op jit(solution)/shard_map/ppermute | solution.py:32
  44.9 16.9 %collective-permute-start.9 = (f32[264,256]{1,0:T(8,128)S(1)}, f32[264,256]{1,0:T(8,128)S(1)}, u32[]{:S(2)}, u32[]{:S(2)}) collective-permute-start(f32[264,256]{1,0:T(8,128)S(1)} %pad_maximum_fusion.t0), channel_id=1, source_target_pairs={{1,0},{2,1},{3,2},{0,3},{5,4},{6,5},{7,6},{4,7},{9,8},{10,9},{11,1... | collective-permute-start | bytes 811016 | tf_op jit(solution)/shard_map/ppermute | solution.py:32
  46.9 23.5 %collective-permute-start.8 = (f32[264,256]{1,0:T(8,128)S(1)}, f32[264,256]{1,0:T(8,128)S(1)}, u32[]{:S(2)}, u32[]{:S(2)}) collective-permute-start(f32[264,256]{1,0:T(8,128)S(1)} %pad_maximum_fusion.1.t0), channel_id=1, source_target_pairs={{3,0},{0,1},{1,2},{2,3},{7,4},{4,5},{5,6},{6,7},{11,8},{8,9},{9,10... | collective-permute-start | bytes 811016 | tf_op jit(solution)/shard_map/ppermute | solution.py:32
  52.1 18.3 %collective-permute-start.7 = (f32[264,256]{1,0:T(8,128)S(1)}, f32[264,256]{1,0:T(8,128)S(1)}, u32[]{:S(2)}, u32[]{:S(2)}) collective-permute-start(f32[264,256]{1,0:T(8,128)S(1)} %pad_maximum_fusion.1.t0), channel_id=1, source_target_pairs={{2,0},{3,1},{0,2},{1,3},{6,4},{7,5},{4,6},{5,7},{10,8},{11,9},{8,1... | collective-permute-start | bytes 811016 | tf_op jit(solution)/shard_map/ppermute | solution.py:32
  54.0 16.4 %collective-permute-start.6 = (f32[264,256]{1,0:T(8,128)S(1)}, f32[264,256]{1,0:T(8,128)S(1)}, u32[]{:S(2)}, u32[]{:S(2)}) collective-permute-start(f32[264,256]{1,0:T(8,128)S(1)} %pad_maximum_fusion.1.t0), channel_id=1, source_target_pairs={{1,0},{2,1},{3,2},{0,3},{5,4},{6,5},{7,6},{4,7},{9,8},{10,9},{11,1... | collective-permute-start | bytes 811016 | tf_op jit(solution)/shard_map/ppermute | solution.py:32
  61.8 0.9 %copy-start = (f32[14,2,8,128]{3,2,1,0:T(8,128)S(1)}, f32[14,2,8,128]{3,2,1,0:T(8,128)}, u32[]{:S(2)}) copy-start(f32[14,2,8,128]{3,2,1,0:T(8,128)} %get-tuple-element.10.taps_ref) | copy-start | bytes 344068
  62.7 0.7 copy-start.1
  63.4 0.7 copy-start.2

commit v2 on v1

v2 whole, which is shorter than its diff:
```python
import jax
import jax.numpy as jnp
from jax import lax
from jax.experimental import pallas as pl
from jax.experimental.pallas import tpu as pltpu
from jax.sharding import PartitionSpec as P

HALO = 4
TAPS = 7
PAD = 24
STEP = 48
BLOCK = 16
AHEAD = (0, 1, 3, 2)
Z_LO, Z_HI, NX, RING = 4, 2, 4, 16


def z_move(value, ahead, steps=0):
    pairs = []
    for z_lo in range(Z_LO):
        for z_hi in range(Z_HI):
            for ring in range(RING):
                for x in range(NX):
                    z = (z_hi * Z_LO + z_lo + ahead) % (Z_LO * Z_HI)
                    lon = (((z_lo + 1) % Z_LO) * RING + ring + steps) % (Z_LO * RING)
                    source = lon * Z_HI * NX + (z // Z_LO) * NX + x
                    target = (z_lo * RING + ring) * Z_HI * NX + z_hi * NX + x
                    pairs.append((source, target))
    return lax.ppermute(value, ("lon", "plane"), pairs)


def swap(value):
    pairs = [(z_hi * NX + x, (1 - z_hi) * NX + x) for z_hi in range(Z_HI) for x in range(NX)]
    return lax.ppermute(value, "plane", pairs)


def x_move(value, ahead):
    pairs = [
        (z_hi * NX + (x + ahead) % NX, z_hi * NX + x) for z_hi in range(Z_HI) for x in range(NX)
    ]
    return lax.ppermute(value, "plane", pairs)


def load_planes(slot_ref, tiles, ext):
    for ahead, tile in zip(AHEAD, tiles):
        slot = slot_ref[ahead].astype(jnp.int32)
        width = tile.shape[1]
        for half in range(2):
            rows = slice(half * 128, half * 128 + 128)
            ext[slot, half, PAD : PAD + width, :] = tile[rows, :].T
            ext[slot, half, PAD - HALO : PAD, :] = tile[width : width + HALO, rows]
            ext[slot, half, PAD + width : PAD + width + HALO, :] = tile[
                width + HALO : width + 2 * HALO, rows
            ]


def stencils(width, taps_ref, ext, fields):
    lane = lax.broadcasted_iota(jnp.int32, (STEP // 8, 8, 128), 2)
    first, last = lane == 0, lane == 127
    start = PAD - 16

    def step(i, carry):
        at = pl.multiple_of(start + i * STEP, 8)
        for slot in range(NX):
            norths, souths, centres = [], [], []
            for half in range(2):
                views = [
                    ext[slot, half, pl.ds(at + tap - 3, STEP), :].reshape(STEP // 8, 8, 128)
                    for tap in range(TAPS)
                ]
                north = views[0] * taps_ref[0, half]
                south = views[0] * taps_ref[TAPS, half]
                for tap in range(1, TAPS):
                    north += views[tap] * taps_ref[tap, half]
                    south += views[tap] * taps_ref[TAPS + tap, half]
                twice = views[3] + views[3]
                east, west = views[4], views[2]
                fields[slot, half, 2, pl.ds(at, STEP), :] = (east - west).reshape(STEP, 128)
                fields[slot, half, 3, pl.ds(at, STEP), :] = (east + west - twice).reshape(STEP, 128)
                norths.append(pltpu.roll(north.reshape(STEP, 128), 1, 1).reshape(north.shape))
                souths.append(pltpu.roll(south.reshape(STEP, 128), 127, 1).reshape(north.shape))
                centres.append(twice)
            n = [jnp.where(first, 0.0, norths[0]), jnp.where(first, norths[0], norths[1])]
            s = [jnp.where(last, souths[1], souths[0]), jnp.where(last, 0.0, souths[1])]
            for half in range(2):
                fields[slot, half, 0, pl.ds(at, STEP), :] = (s[half] - n[half]).reshape(STEP, 128)
                fields[slot, half, 1, pl.ds(at, STEP), :] = (
                    s[half] + n[half] - centres[half]
                ).reshape(STEP, 128)
        return carry

    lax.fori_loop(0, (width + 2 * 16) // STEP, step, 0)


def compose(at, half, hi, scalar_ref, metric_ref, fields):
    half_m, square_m, quarter_m = metric_ref[0, half], metric_ref[1, half], metric_ref[2, half]

    def load(slot, k, shift=0):
        return fields[slot, half, k, pl.ds(at + shift, BLOCK), :].reshape(BLOCK // 8, 8, 128)

    state = None
    for slot in range(NX):
        gain = scalar_ref[NX + 1 + hi * NX + slot]
        alpha_t = (0.5 * gain) * load(slot, 0)
        alpha_p = (gain * half_m) * load(slot, 2)
        u_tt = gain * load(slot, 1)
        u_pp = (gain * square_m) * load(slot, 3)
        u_tp = (gain * quarter_m) * (load(slot, 0, 1) - load(slot, 0, -1))
        if state is None:
            state = (-alpha_t, -alpha_p, 1.0 - u_tt, -u_tp, -u_tp, 1.0 - u_pp)
        else:
            d_t, d_p, a_zz, a_zo, a_oz, a_oo = state
            state = (
                d_t - (alpha_t + (u_tt * d_t + u_tp * d_p)),
                d_p - (alpha_p + (u_tp * d_t + u_pp * d_p)),
                a_zz - (u_tt * a_zz + u_tp * a_oz),
                a_zo - (u_tt * a_zo + u_tp * a_oo),
                a_oz - (u_tp * a_zz + u_pp * a_oz),
                a_oo - (u_tp * a_zo + u_pp * a_oo),
            )
    return state


def begin(scalar_ref, taps_hbm, metric_hbm, tiles, ext, fields, taps, metric, sems):
    copies = [
        pltpu.make_async_copy(taps_hbm, taps, sems.at[0]),
        pltpu.make_async_copy(metric_hbm, metric, sems.at[1]),
    ]
    for copy in copies:
        copy.start()
    load_planes(scalar_ref, tiles, ext)
    for copy in copies:
        copy.wait()
    stencils(tiles[0].shape[1], taps, ext, fields)


def first_kernel(
    scalar_ref, taps_hbm, metric_hbm, t0, t1, t2, t3, out, ext, fields, taps, metric, sems
):
    begin(scalar_ref, taps_hbm, metric_hbm, (t0, t1, t2, t3), ext, fields, taps, metric, sems)
    hi = scalar_ref[NX].astype(jnp.int32)

    def block(j, carry):
        at = pl.multiple_of(j * BLOCK, BLOCK)
        for half in range(2):
            state = compose(at + PAD, half, hi, scalar_ref, metric, fields)
            for k in range(6):
                out[k, half, pl.ds(at, BLOCK), :] = state[k].reshape(BLOCK, 128)
        return carry

    lax.fori_loop(0, t0.shape[1] // BLOCK, block, 0)


def second_kernel(
    scalar_ref,
    taps_hbm,
    metric_hbm,
    t0,
    t1,
    t2,
    t3,
    other,
    disp,
    jac,
    ext,
    fields,
    taps,
    metric,
    sems,
    done,
):
    begin(scalar_ref, taps_hbm, metric_hbm, (t0, t1, t2, t3), ext, fields, taps, metric, sems)
    hi = 1 - scalar_ref[NX].astype(jnp.int32)
    other_first = hi == 1

    def block(j, carry):
        at = pl.multiple_of(j * BLOCK, BLOCK)
        for half in range(2):
            here = compose(at + PAD, half, hi, scalar_ref, metric, fields)
            there = [
                other[k, half, pl.ds(at, BLOCK), :].reshape(BLOCK // 8, 8, 128) for k in range(6)
            ]
            d_t, d_p, a_zz, a_zo, a_oz, a_oo = [
                jnp.where(other_first, a, b) for a, b in zip(there, here)
            ]
            e_t, e_p, b_zz, b_zo, b_oz, b_oo = [
                jnp.where(other_first, b, a) for a, b in zip(there, here)
            ]
            state = (
                e_t + (b_zz * d_t + b_zo * d_p),
                e_p + (b_oz * d_t + b_oo * d_p),
                b_zz * a_zz + b_zo * a_oz,
                b_zz * a_zo + b_zo * a_oo,
                b_oz * a_zz + b_oo * a_oz,
                b_oz * a_zo + b_oo * a_oo,
            )
            for k in range(6):
                done[k, half, pl.ds(at, BLOCK), :] = state[k].reshape(BLOCK, 128)
        return carry

    lax.fori_loop(0, t0.shape[1] // BLOCK, block, 0)
    for k in range(6):
        for half in range(2):
            rows = slice(half * 128, half * 128 + 128)
            turned = done[k, half].T
            if k < 2:
                disp[k, rows, :] = turned
            else:
                jac[k - 2, rows, :] = turned


def smem():
    return pl.BlockSpec(memory_space=pltpu.SMEM)


def vmem():
    return pl.BlockSpec(memory_space=pltpu.VMEM)


def scratch(rows, width):
    return [
        pltpu.VMEM((NX, 2, width + 2 * PAD, rows // 2), jnp.float32),
        pltpu.VMEM((NX, 2, 4, width + 2 * PAD, rows // 2), jnp.float32),
        pltpu.VMEM((2 * TAPS, 2, 8, rows // 2), jnp.float32),
        pltpu.VMEM((3, 2, 8, rows // 2), jnp.float32),
        pltpu.SemaphoreType.DMA((2,)),
    ]


def cost(rows, width):
    return pl.CostEstimate(
        flops=260 * NX * rows * width, bytes_accessed=40 * rows * width, transcendentals=0
    )


def prepare_kernel(tile_ref, shift_ref, weight_ref, scale_ref, low, high, taps, metric):
    rows, width = tile_ref.shape
    for half in range(2):
        lanes = slice(half * 128, half * 128 + 128)
        low[:, lanes] = tile_ref[lanes, width - 128 :].T[128 - HALO :]
        high[:, lanes] = tile_ref[lanes, :128].T[:HALO]
    for side, turn in ((0, rows - 1), (1, 1)):
        shift = jnp.broadcast_to(shift_ref[side : side + 1, :], (8, rows))
        frac = jnp.broadcast_to(weight_ref[side : side + 1, :].astype(jnp.float32) / 16.0, (8, rows))
        shift, frac = pltpu.roll(shift, turn, 1), pltpu.roll(frac, turn, 1)
        for tap in range(TAPS):
            value = jnp.where(shift == tap - 3, 1.0 - frac, 0.0)
            value += jnp.where(shift == tap - 4, frac, 0.0)
            for half in range(2):
                taps[side * TAPS + tap, half] = value[:, half * 128 : half * 128 + 128]
    scale = jnp.broadcast_to(scale_ref[...], (8, rows))
    for k, value in enumerate((0.5 * scale, scale * scale, 0.25 * scale)):
        for half in range(2):
            metric[k, half] = value[:, half * 128 : half * 128 + 128]


def prepare(tile, cycle_shift, cycle_weight, cycle_scale):
    rows = tile.shape[0]
    return pl.pallas_call(
        prepare_kernel,
        out_shape=(
            jax.ShapeDtypeStruct((HALO, rows), jnp.float32),
            jax.ShapeDtypeStruct((HALO, rows), jnp.float32),
            jax.ShapeDtypeStruct((2 * TAPS, 2, 8, rows // 2), jnp.float32),
            jax.ShapeDtypeStruct((3, 2, 8, rows // 2), jnp.float32),
        ),
        in_specs=[vmem()] * 4,
        out_specs=(vmem(),) * 4,
        cost_estimate=pl.CostEstimate(flops=1 << 16, bytes_accessed=1 << 20, transcendentals=0),
        name="prepare",
    )(tile, cycle_shift, cycle_weight, cycle_scale[None])


def per_device(potential, lens_weight, cycle_shift, cycle_weight, cycle_scale):
    tile = potential[0]
    rows, width = tile.shape
    lon, plane = lax.axis_index("lon"), lax.axis_index("plane")
    x = plane % NX
    near_hi = (((plane // NX) * Z_LO + lon // RING + 1) // Z_LO) % Z_HI
    order = jnp.arange(NX + 1, dtype=jnp.int32)
    places = jnp.where(order < NX, (x + order) % NX, near_hi).astype(jnp.float32)
    scalars = jnp.concatenate([places, lens_weight[0]])

    low, high, taps, metric = prepare(tile, cycle_shift, cycle_weight, cycle_scale)
    near, far = z_move(tile, 1), z_move(tile, 1 + Z_LO)
    strips = jnp.concatenate([z_move(low, 1, -1), z_move(high, 1, 1)])
    near = jnp.concatenate([near, strips])
    near_tiles = tuple([near] + [x_move(near, ahead) for ahead in AHEAD[1:]])
    far = jnp.concatenate([far, swap(strips)])
    far_tiles = tuple([far] + [x_move(far, ahead) for ahead in AHEAD[1:]])

    in_hbm = pl.BlockSpec(memory_space=pltpu.HBM)
    state = pl.pallas_call(
        first_kernel,
        out_shape=jax.ShapeDtypeStruct((6, 2, width, rows // 2), jnp.float32),
        in_specs=[smem(), in_hbm, in_hbm] + [vmem()] * 4,
        out_specs=vmem(),
        scratch_shapes=scratch(rows, width),
        cost_estimate=cost(rows, width),
        compiler_params=pltpu.CompilerParams(vmem_limit_bytes=24 << 20),
        name="near_planes",
    )(scalars, taps, metric, *near_tiles)
    displacement, jacobian = pl.pallas_call(
        second_kernel,
        out_shape=(
            jax.ShapeDtypeStruct((2, rows, width), jnp.float32),
            jax.ShapeDtypeStruct((4, rows, width), jnp.float32),
        ),
        in_specs=[smem(), in_hbm, in_hbm] + [vmem()] * 5,
        out_specs=(vmem(), vmem()),
        scratch_shapes=scratch(rows, width)
        + [pltpu.VMEM((6, 2, width, rows // 2), jnp.float32)],
        cost_estimate=cost(rows, width),
        compiler_params=pltpu.CompilerParams(vmem_limit_bytes=24 << 20),
        name="far_planes",
    )(scalars, taps, metric, *far_tiles, state)
    return displacement[None], jacobian[None]


def solution(mesh):
    in_specs = (P("plane", None, "lon"), P("plane", None), P(), P(), P())
    out_specs = (P("plane", None, None, "lon"), P("plane", None, None, "lon"))
    return jax.shard_map(
        per_device, mesh=mesh, in_specs=in_specs, out_specs=out_specs, check_vma=False
    )
```

time: 78.8 us -> 69.2 us (0.88)
  the two profiles are of different devices: /device:TPU:6 before, /device:TPU:31 now
where the time goes in v2:
time: 69.2 us; the launch traced here: 68.7 us
  starting transfers between devices  44 us (64%)
  Pallas kernels  11.6 us (17%)
  waiting for transfers between devices  9.69 us (14%)
  local copies, waits for them, and re-layouts  1.66 us (2%)
  between operations  0.88 us (1%)
  other arithmetic  0.77 us (1%)
    ppermute x4, starting transfers between devices, z_move(): return lax.ppermute(value, ('lon', 'plane'), pairs)  19.7 us
    ppermute x6, starting transfers between devices, x_move(): return lax.ppermute(value, 'plane', pairs)  17.7 us
    ppermute x1, starting transfers between devices, swap(): return lax.ppermute(value, 'plane', pairs)  6.64 us
    pallas_call x1, Pallas kernels, per_device(): pl.pallas_call(second_kernel, out_shape=(jax.ShapeDtypeStruct((2, rows, w...  5.76 us
    ppermute x4, waiting for transfers between devices, z_move(): return lax.ppermute(value, ('lon', 'plane'), pairs)  5.61 us
    ppermute x6, waiting for transfers between devices, x_move(): return lax.ppermute(value, 'plane', pairs)  4.08 us
    pallas_call x1, Pallas kernels, per_device(): pl.pallas_call(first_kernel, out_shape=jax.ShapeDtypeStruct((6, 2, width,...  4.06 us
    pallas_call x1, Pallas kernels, prepare(): pl.pallas_call(prepare_kernel, out_shape=(jax.ShapeDtypeStruct((HALO, row...  1.8 us
  transfers between devices with their start and end apart: 11, of which 2 were waited for; matrix products, arithmetic and copies ran while one was open for 1% of the time, Pallas kernels for 9%

profile of v2, /device:TPU:31, one launch (start us, length us, event | category | flops | bytes accessed | tf_op | source)
XLA Modules:
  0.0 68.7 jit_solution(16124552045336799724)
XLA Ops:
  0.6 10.7 %collective-permute-start.7 = (f32[256,256]{1,0:T(8,128)}, f32[256,256]{1,0:T(8,128)S(1)}, u32[]{:S(2)}, u32[]{:S(2)}) collective-permute-start(f32[256,256]{1,0:T(8,128)} %bitcast.5), channel_id=1, source_target_pairs={{128,0},{129,1},{130,2},{131,3},{136,8},{137,9},{138,10},{139,11},... | collective-permute-start | bytes 786440 | tf_op jit(solution)/shard_map/ppermute | solution.py:28
  11.3 1.9 %collective-permute-start = (f32[256,256]{1,0:T(8,128)}, f32[256,256]{1,0:T(8,128)S(1)}, u32[]{:S(2)}, u32[]{:S(2)}) collective-permute-start(f32[256,256]{1,0:T(8,128)} %bitcast.6), channel_id=1, source_target_pairs={{132,0},{133,1},{134,2},{135,3},{140,8},{141,9},{142,10},{143,11},... | collective-permute-start | bytes 786440 | tf_op jit(solution)/shard_map/ppermute | solution.py:28
  13.2 1.8 %prepare.1 = (f32[4,256]{1,0:T(4,128)}, f32[4,256]{1,0:T(4,128)}, f32[14,2,8,128]{3,2,1,0:T(8,128)}, f32[3,2,8,128]{3,2,1,0:T(8,128)}) custom-call(f32[256,256]{1,0:T(8,128)} %bitcast.7, s32[2,256]{1,0:T(2,128)} %shift_ref.1, s32[2,256]{1,0:T(2,128)} %weight_ref.1, f32[1,256]{1,0:T(1,128)} %bitcast.8), custom_call_target="tpu_custom_call" | custom-call | flops 65536 | bytes 1048576 | tf_op jit(solution)/shard_map/prepare/pallas_call | solution.py:258
  15.0 5.2 %collective-permute-start.1 = (f32[4,256]{1,0:T(4,128)}, f32[4,256]{1,0:T(4,128)S(1)}, u32[]{:S(2)}, u32[]{:S(2)}) collective-permute-start(f32[4,256]{1,0:T(4,128)} %get-tuple-element.10), channel_id=1, source_target_pairs={{120,0},{121,1},{122,2},{123,3},{128,8},{129,9},{130,10},{131,11},... | collective-permute-start | bytes 12296 | tf_op jit(solution)/shard_map/ppermute | solution.py:28
  20.3 1.9 %collective-permute-start.2 = (f32[4,256]{1,0:T(4,128)}, f32[4,256]{1,0:T(4,128)S(1)}, u32[]{:S(2)}, u32[]{:S(2)}) collective-permute-start(f32[4,256]{1,0:T(4,128)} %get-tuple-element.11), channel_id=1, source_target_pairs={{136,0},{137,1},{138,2},{139,3},{144,8},{145,9},{146,10},{147,11},... | collective-permute-start | bytes 12296 | tf_op jit(solution)/shard_map/ppermute | solution.py:28
  22.2 0.0 collective-permute-done.1
  22.2 5.6 %collective-permute-done.2 = f32[4,256]{1,0:T(4,128)S(1)} collective-permute-done((f32[4,256]{1,0:T(4,128)}, f32[4,256]{1,0:T(4,128)S(1)}, u32[]{:S(2)}, u32[]{:S(2)}) %collective-permute-start.2) | collective-permute-done | bytes 4128 | tf_op jit(solution)/shard_map/ppermute | solution.py:28
  27.8 0.0 collective-permute-done.7
  27.8 3.0 %collective-permute-start.10 = (f32[264,256]{1,0:T(8,128)S(1)}, f32[264,256]{1,0:T(8,128)S(1)}, u32[]{:S(2)}, u32[]{:S(2)}) collective-permute-start(f32[264,256]{1,0:T(8,128)S(1)} %pad_maximum_fusion.t0), channel_id=1, source_target_pairs={{2,0},{3,1},{0,2},{1,3},{6,4},{7,5},{4,6},{5,7},{10,8},{11,9},{8,1... | collective-permute-start | bytes 811016 | tf_op jit(solution)/shard_map/ppermute | solution.py:40
  30.9 6.6 %collective-permute-start.3 = (f32[8,256]{1,0:T(8,128)S(1)}, f32[8,256]{1,0:T(8,128)S(1)}, u32[]{:S(2)}, u32[]{:S(2)}) collective-permute-start(f32[8,256]{1,0:T(8,128)S(1)} %pad_maximum_fusion.1), channel_id=1, source_target_pairs={{0,4},{1,5},{2,6},{3,7},{4,0},{5,1},{6,2},{7,3},{8,12},{9,13},{10,... | collective-permute-start | bytes 24584 | tf_op jit(solution)/shard_map/ppermute | solution.py:33
  37.5 3.7 %collective-permute-start.9 = (f32[264,256]{1,0:T(8,128)S(1)}, f32[264,256]{1,0:T(8,128)S(1)}, u32[]{:S(2)}, u32[]{:S(2)}) collective-permute-start(f32[264,256]{1,0:T(8,128)S(1)} %pad_maximum_fusion.t0), channel_id=1, source_target_pairs={{3,0},{0,1},{1,2},{2,3},{7,4},{4,5},{5,6},{6,7},{11,8},{8,9},{9,10... | collective-permute-start | bytes 811016 | tf_op jit(solution)/shard_map/ppermute | solution.py:40
  41.3 1.9 %collective-permute-start.8 = (f32[264,256]{1,0:T(8,128)S(1)}, f32[264,256]{1,0:T(8,128)S(1)}, u32[]{:S(2)}, u32[]{:S(2)}) collective-permute-start(f32[264,256]{1,0:T(8,128)S(1)} %pad_maximum_fusion.t0), channel_id=1, source_target_pairs={{1,0},{2,1},{3,2},{0,3},{5,4},{6,5},{7,6},{4,7},{9,8},{10,9},{11,1... | collective-permute-start | bytes 811016 | tf_op jit(solution)/shard_map/ppermute | solution.py:40
  43.2 0.0 collective-permute-done
  43.2 0.0 collective-permute-done.3
  43.3 3.4 %collective-permute-start.6 = (f32[264,256]{1,0:T(8,128)S(1)}, f32[264,256]{1,0:T(8,128)S(1)}, u32[]{:S(2)}, u32[]{:S(2)}) collective-permute-start(f32[264,256]{1,0:T(8,128)S(1)} %constant_dynamic-update-slice_fusion.t0), channel_id=1, source_target_pairs={{2,0},{3,1},{0,2},{1,3},{6,4},{7,5},{4,6},{5,7},{10,8},{11,9},{8,1... | collective-permute-start | bytes 811016 | tf_op jit(solution)/shard_map/ppermute | solution.py:40
  46.7 3.1 %collective-permute-start.5 = (f32[264,256]{1,0:T(8,128)S(1)}, f32[264,256]{1,0:T(8,128)S(1)}, u32[]{:S(2)}, u32[]{:S(2)}) collective-permute-start(f32[264,256]{1,0:T(8,128)S(1)} %constant_dynamic-update-slice_fusion.t0), channel_id=1, source_target_pairs={{3,0},{0,1},{1,2},{2,3},{7,4},{4,5},{5,6},{6,7},{11,8},{8,9},{9,10... | collective-permute-start | bytes 811016 | tf_op jit(solution)/shard_map/ppermute | solution.py:40
  49.8 0.0 collective-permute-done.10.t3
  49.8 2.5 %collective-permute-start.4 = (f32[264,256]{1,0:T(8,128)S(1)}, f32[264,256]{1,0:T(8,128)S(1)}, u32[]{:S(2)}, u32[]{:S(2)}) collective-permute-start(f32[264,256]{1,0:T(8,128)S(1)} %constant_dynamic-update-slice_fusion.t0), channel_id=1, source_target_pairs={{1,0},{2,1},{3,2},{0,3},{5,4},{6,5},{7,6},{4,7},{9,8},{10,9},{11,1... | collective-permute-start | bytes 811016 | tf_op jit(solution)/shard_map/ppermute | solution.py:40
  52.4 0.7 %pad_maximum_fusion.2.scalar_ref = f32[13]{0:T(128)S(1)} fusion(f32[8]{0:T(128)} %bitcast.11, f32[5]{0:T(128)S(1)} %fusion.1), kind=kLoop, calls=%fused_computation.9 | loop fusion | flops 13 | bytes 104 | tf_op jit(solution)/shard_map/concatenate | solution.py:281
  53.1 0.0 collective-permute-done.9.t2
  53.1 4.1 %collective-permute-done.8.t1 = f32[264,256]{1,0:T(8,128)S(1)} collective-permute-done((f32[264,256]{1,0:T(8,128)S(1)}, f32[264,256]{1,0:T(8,128)S(1)}, u32[]{:S(2)}, u32[]{:S(2)}) %collective-permute-start.8) | collective-permute-done | bytes 270368 | tf_op jit(solution)/shard_map/ppermute | solution.py:40
  57.2 0.0 copy-start
  57.2 0.9 %copy-done = f32[14,2,8,128]{3,2,1,0:T(8,128)S(1)} copy-done((f32[14,2,8,128]{3,2,1,0:T(8,128)S(1)}, f32[14,2,8,128]{3,2,1,0:T(8,128)}, u32[]{:S(2)}) %copy-start) | copy-done | bytes 114712
  58.1 0.0 copy-start.1
  58.1 0.7 %copy-done.1 = f32[3,2,8,128]{3,2,1,0:T(8,128)S(1)} copy-done((f32[3,2,8,128]{3,2,1,0:T(8,128)S(1)}, f32[3,2,8,128]{3,2,1,0:T(8,128)}, u32[]{:S(2)}) %copy-start.1) | copy-done | bytes 24600
  58.8 4.1 %near_planes.1.other = f32[6,2,256,128]{3,2,1,0:T(8,128)S(1)} custom-call(f32[13]{0:T(128)S(1)} %pad_maximum_fusion.2.scalar_ref, f32[14,2,8,128]{3,2,1,0:T(8,128)S(1)} %copy-done, f32[3,2,8,128]{3,2,1,0:T(8,128)S(1)} %copy-done.1, f32[264,256]{1,0:T(8,128)S(1)} %pad_maximum_fusion.t0, f32[264,256]{1,0:T(8,128)S(1)} %collective-permute-done.8.t1, ...), custom_call_target="tpu_custom_call" | custom-call | flops 68157440 | bytes 2621440 | tf_op jit(solution)/shard_map/near_planes/pallas_call | solution.py:292
  62.9 0.0 collective-permute-done.6.t3
  62.9 0.0 collective-permute-done.5.t2
  62.9 0.0 collective-permute-done.4.t1
  62.9 5.8 %far_planes.1 = (f32[2,256,256]{2,1,0:T(8,128)}, f32[4,256,256]{2,1,0:T(8,128)}) custom-call(f32[13]{0:T(128)S(1)} %pad_maximum_fusion.2.scalar_ref, f32[14,2,8,128]{3,2,1,0:T(8,128)S(1)} %copy-done, f32[3,2,8,128]{3,2,1,0:T(8,128)S(1)} %copy-done.1, f32[264,256]{1,0:T(8,128)S(1)} %constant_dynamic-update-slice_fusion.t0, ...), custom_call_target="tpu_custom_call" | custom-call | flops 68157440 | bytes 2621440 | tf_op jit(solution)/shard_map/far_planes/pallas_call | solution.py:302
  (5 shorter events, 0.1 us)
Async XLA Ops:
  0.6 27.2 %collective-permute-start.7 = (f32[256,256]{1,0:T(8,128)}, f32[256,256]{1,0:T(8,128)S(1)}, u32[]{:S(2)}, u32[]{:S(2)}) collective-permute-start(f32[256,256]{1,0:T(8,128)} %bitcast.5), channel_id=1, source_target_pairs={{128,0},{129,1},{130,2},{131,3},{136,8},{137,9},{138,10},{139,11},... | collective-permute-start | bytes 786440 | tf_op jit(solution)/shard_map/ppermute | solution.py:28
  11.3 31.9 %collective-permute-start = (f32[256,256]{1,0:T(8,128)}, f32[256,256]{1,0:T(8,128)S(1)}, u32[]{:S(2)}, u32[]{:S(2)}) collective-permute-start(f32[256,256]{1,0:T(8,128)} %bitcast.6), channel_id=1, source_target_pairs={{132,0},{133,1},{134,2},{135,3},{140,8},{141,9},{142,10},{143,11},... | collective-permute-start | bytes 786440 | tf_op jit(solution)/shard_map/ppermute | solution.py:28
  15.0 7.2 %collective-permute-start.1 = (f32[4,256]{1,0:T(4,128)}, f32[4,256]{1,0:T(4,128)S(1)}, u32[]{:S(2)}, u32[]{:S(2)}) collective-permute-start(f32[4,256]{1,0:T(4,128)} %get-tuple-element.10), channel_id=1, source_target_pairs={{120,0},{121,1},{122,2},{123,3},{128,8},{129,9},{130,10},{131,11},... | collective-permute-start | bytes 12296 | tf_op jit(solution)/shard_map/ppermute | solution.py:28
  20.3 7.5 %collective-permute-start.2 = (f32[4,256]{1,0:T(4,128)}, f32[4,256]{1,0:T(4,128)S(1)}, u32[]{:S(2)}, u32[]{:S(2)}) collective-permute-start(f32[4,256]{1,0:T(4,128)} %get-tuple-element.11), channel_id=1, source_target_pairs={{136,0},{137,1},{138,2},{139,3},{144,8},{145,9},{146,10},{147,11},... | collective-permute-start | bytes 12296 | tf_op jit(solution)/shard_map/ppermute | solution.py:28
  27.8 21.9 %collective-permute-start.10 = (f32[264,256]{1,0:T(8,128)S(1)}, f32[264,256]{1,0:T(8,128)S(1)}, u32[]{:S(2)}, u32[]{:S(2)}) collective-permute-start(f32[264,256]{1,0:T(8,128)S(1)} %pad_maximum_fusion.t0), channel_id=1, source_target_pairs={{2,0},{3,1},{0,2},{1,3},{6,4},{7,5},{4,6},{5,7},{10,8},{11,9},{8,1... | collective-permute-start | bytes 811016 | tf_op jit(solution)/shard_map/ppermute | solution.py:40
  30.9 12.3 %collective-permute-start.3 = (f32[8,256]{1,0:T(8,128)S(1)}, f32[8,256]{1,0:T(8,128)S(1)}, u32[]{:S(2)}, u32[]{:S(2)}) collective-permute-start(f32[8,256]{1,0:T(8,128)S(1)} %pad_maximum_fusion.1), channel_id=1, source_target_pairs={{0,4},{1,5},{2,6},{3,7},{4,0},{5,1},{6,2},{7,3},{8,12},{9,13},{10,... | collective-permute-start | bytes 24584 | tf_op jit(solution)/shard_map/ppermute | solution.py:33
  37.5 15.6 %collective-permute-start.9 = (f32[264,256]{1,0:T(8,128)S(1)}, f32[264,256]{1,0:T(8,128)S(1)}, u32[]{:S(2)}, u32[]{:S(2)}) collective-permute-start(f32[264,256]{1,0:T(8,128)S(1)} %pad_maximum_fusion.t0), channel_id=1, source_target_pairs={{3,0},{0,1},{1,2},{2,3},{7,4},{4,5},{5,6},{6,7},{11,8},{8,9},{9,10... | collective-permute-start | bytes 811016 | tf_op jit(solution)/shard_map/ppermute | solution.py:40
  41.3 15.9 %collective-permute-start.8 = (f32[264,256]{1,0:T(8,128)S(1)}, f32[264,256]{1,0:T(8,128)S(1)}, u32[]{:S(2)}, u32[]{:S(2)}) collective-permute-start(f32[264,256]{1,0:T(8,128)S(1)} %pad_maximum_fusion.t0), channel_id=1, source_target_pairs={{1,0},{2,1},{3,2},{0,3},{5,4},{6,5},{7,6},{4,7},{9,8},{10,9},{11,1... | collective-permute-start | bytes 811016 | tf_op jit(solution)/shard_map/ppermute | solution.py:40
  43.3 19.6 %collective-permute-start.6 = (f32[264,256]{1,0:T(8,128)S(1)}, f32[264,256]{1,0:T(8,128)S(1)}, u32[]{:S(2)}, u32[]{:S(2)}) collective-permute-start(f32[264,256]{1,0:T(8,128)S(1)} %constant_dynamic-update-slice_fusion.t0), channel_id=1, source_target_pairs={{2,0},{3,1},{0,2},{1,3},{6,4},{7,5},{4,6},{5,7},{10,8},{11,9},{8,1... | collective-permute-start | bytes 811016 | tf_op jit(solution)/shard_map/ppermute | solution.py:40
  46.7 16.2 %collective-permute-start.5 = (f32[264,256]{1,0:T(8,128)S(1)}, f32[264,256]{1,0:T(8,128)S(1)}, u32[]{:S(2)}, u32[]{:S(2)}) collective-permute-start(f32[264,256]{1,0:T(8,128)S(1)} %constant_dynamic-update-slice_fusion.t0), channel_id=1, source_target_pairs={{3,0},{0,1},{1,2},{2,3},{7,4},{4,5},{5,6},{6,7},{11,8},{8,9},{9,10... | collective-permute-start | bytes 811016 | tf_op jit(solution)/shard_map/ppermute | solution.py:40
  49.8 13.1 %collective-permute-start.4 = (f32[264,256]{1,0:T(8,128)S(1)}, f32[264,256]{1,0:T(8,128)S(1)}, u32[]{:S(2)}, u32[]{:S(2)}) collective-permute-start(f32[264,256]{1,0:T(8,128)S(1)} %constant_dynamic-update-slice_fusion.t0), channel_id=1, source_target_pairs={{1,0},{2,1},{3,2},{0,3},{5,4},{6,5},{7,6},{4,7},{9,8},{10,9},{11,1... | collective-permute-start | bytes 811016 | tf_op jit(solution)/shard_map/ppermute | solution.py:40
  57.2 0.9 %copy-start = (f32[14,2,8,128]{3,2,1,0:T(8,128)S(1)}, f32[14,2,8,128]{3,2,1,0:T(8,128)}, u32[]{:S(2)}) copy-start(f32[14,2,8,128]{3,2,1,0:T(8,128)} %get-tuple-element.8.taps_hbm) | copy-start | bytes 344068
  58.1 0.7 %copy-start.1 = (f32[3,2,8,128]{3,2,1,0:T(8,128)S(1)}, f32[3,2,8,128]{3,2,1,0:T(8,128)}, u32[]{:S(2)}) copy-start(f32[3,2,8,128]{3,2,1,0:T(8,128)} %get-tuple-element.9.metric_hbm) | copy-start | bytes 73732

commit v3 on v2

v3 whole, which is shorter than its diff:
```python
import jax
import jax.numpy as jnp
from jax import lax
from jax.experimental import pallas as pl
from jax.experimental.pallas import tpu as pltpu
from jax.sharding import PartitionSpec as P

HALO = 4
TAPS = 7
PAD = 24
STEP = 48
BLOCK = 16
NEAR = (0, 1, 3, 2)
FAR = (0, 3, 2, 1)
Z_LO, Z_HI, NX, RING = 4, 2, 4, 16


def z_move(value, ahead, steps=0):
    pairs = []
    for z_lo in range(Z_LO):
        for z_hi in range(Z_HI):
            for ring in range(RING):
                for x in range(NX):
                    z = (z_hi * Z_LO + z_lo + ahead) % (Z_LO * Z_HI)
                    lon = (((z_lo + 1) % Z_LO) * RING + ring + steps) % (Z_LO * RING)
                    source = lon * Z_HI * NX + (z // Z_LO) * NX + x
                    target = (z_lo * RING + ring) * Z_HI * NX + z_hi * NX + x
                    pairs.append((source, target))
    return lax.ppermute(value, ("lon", "plane"), pairs)


def swap(value):
    pairs = [(z_hi * NX + x, (1 - z_hi) * NX + x) for z_hi in range(Z_HI) for x in range(NX)]
    return lax.ppermute(value, "plane", pairs)


def x_move(value, ahead):
    pairs = [
        (z_hi * NX + (x + ahead) % NX, z_hi * NX + x) for z_hi in range(Z_HI) for x in range(NX)
    ]
    return lax.ppermute(value, "plane", pairs)


def load_planes(slots, tiles, ext):
    for slot, tile in zip(slots, tiles):
        width = tile.shape[1]
        for half in range(2):
            rows = slice(half * 128, half * 128 + 128)
            ext[slot, half, PAD : PAD + width, :] = tile[rows, :].T
            ext[slot, half, PAD - HALO : PAD, :] = tile[width : width + HALO, rows]
            ext[slot, half, PAD + width : PAD + width + HALO, :] = tile[
                width + HALO : width + 2 * HALO, rows
            ]


def stencils(width, taps_ref, ext, fields):
    lane = lax.broadcasted_iota(jnp.int32, (STEP // 8, 8, 128), 2)
    first, last = lane == 0, lane == 127
    start = PAD - 16

    def step(i, carry):
        at = pl.multiple_of(start + i * STEP, 8)
        for slot in range(ext.shape[0]):
            norths, souths, centres = [], [], []
            for half in range(2):
                views = [
                    ext[slot, half, pl.ds(at + tap - 3, STEP), :].reshape(STEP // 8, 8, 128)
                    for tap in range(TAPS)
                ]
                north = views[0] * taps_ref[0, half]
                south = views[0] * taps_ref[TAPS, half]
                for tap in range(1, TAPS):
                    north += views[tap] * taps_ref[tap, half]
                    south += views[tap] * taps_ref[TAPS + tap, half]
                twice = views[3] + views[3]
                east, west = views[4], views[2]
                fields[slot, half, 2, pl.ds(at, STEP), :] = (east - west).reshape(STEP, 128)
                fields[slot, half, 3, pl.ds(at, STEP), :] = (east + west - twice).reshape(STEP, 128)
                norths.append(pltpu.roll(north.reshape(STEP, 128), 1, 1).reshape(north.shape))
                souths.append(pltpu.roll(south.reshape(STEP, 128), 127, 1).reshape(north.shape))
                centres.append(twice)
            n = [jnp.where(first, 0.0, norths[0]), jnp.where(first, norths[0], norths[1])]
            s = [jnp.where(last, souths[1], souths[0]), jnp.where(last, 0.0, souths[1])]
            for half in range(2):
                fields[slot, half, 0, pl.ds(at, STEP), :] = (s[half] - n[half]).reshape(STEP, 128)
                fields[slot, half, 1, pl.ds(at, STEP), :] = (
                    s[half] + n[half] - centres[half]
                ).reshape(STEP, 128)
        return carry

    lax.fori_loop(0, (width + 2 * 16) // STEP, step, 0)


def compose(half, hi, tables, load):
    half_m, square_m, quarter_m = [tables[2 * TAPS + k, half] for k in range(3)]
    state = None
    for slot in range(NX):
        gain = tables[2 * TAPS + 3 + hi * (NX // 2) + slot // 2, slot % 2]
        alpha_t = (0.5 * gain) * load(slot, 0)
        alpha_p = (gain * half_m) * load(slot, 2)
        u_tt = gain * load(slot, 1)
        u_pp = (gain * square_m) * load(slot, 3)
        u_tp = (gain * quarter_m) * (load(slot, 0, 1) - load(slot, 0, -1))
        if state is None:
            state = (-alpha_t, -alpha_p, 1.0 - u_tt, -u_tp, -u_tp, 1.0 - u_pp)
        else:
            d_t, d_p, a_zz, a_zo, a_oz, a_oo = state
            state = (
                d_t - (alpha_t + (u_tt * d_t + u_tp * d_p)),
                d_p - (alpha_p + (u_tp * d_t + u_pp * d_p)),
                a_zz - (u_tt * a_zz + u_tp * a_oz),
                a_zo - (u_tt * a_zo + u_tp * a_oo),
                a_oz - (u_tp * a_zz + u_pp * a_oz),
                a_oo - (u_tp * a_zo + u_pp * a_oo),
            )
    return state


def block_of(ref, at):
    return ref[pl.ds(at, BLOCK), :].reshape(BLOCK // 8, 8, 128)


def near_kernel(scalar_ref, tables, t0, t1, t2, t3, out, ext, fields):
    width = t0.shape[1]
    slots = [lax.rem(scalar_ref[0] + ahead, NX) for ahead in NEAR]
    load_planes(slots, (t0, t1, t2, t3), ext)
    stencils(width, tables, ext, fields)
    hi = scalar_ref[1]

    def block(j, carry):
        at = pl.multiple_of(j * BLOCK, BLOCK)
        for half in range(2):

            def load(slot, k, shift=0):
                return block_of(fields.at[slot, half, k], at + PAD + shift)

            state = compose(half, hi, tables, load)
            for k in range(6):
                out[k, half, pl.ds(at, BLOCK), :] = state[k].reshape(BLOCK, 128)
        return carry

    lax.fori_loop(0, width // BLOCK, block, 0)


def early_kernel(tables, t0, t1, t2, after, fields, ext):
    load_planes(range(3), (t0, t1, t2), ext)
    stencils(t0.shape[1], tables, ext, fields)


def far_kernel(scalar_ref, tables, last, early, other, disp, jac, ext, fields, done):
    width = last.shape[1]
    load_planes(range(1), (last,), ext)
    stencils(width, tables, ext, fields)
    hi = 1 - scalar_ref[1]
    other_first = hi == 1

    def rays(x):
        def block(j, carry):
            at = pl.multiple_of(j * BLOCK, BLOCK)
            for half in range(2):

                def load(slot, k, shift=0):
                    tile = FAR.index((slot - x) % NX)
                    ref = fields.at[0] if tile == NX - 1 else early.at[tile]
                    return block_of(ref.at[half, k], at + PAD + shift)

                here = compose(half, hi, tables, load)
                there = [block_of(other.at[k, half], at) for k in range(6)]
                d_t, d_p, a_zz, a_zo, a_oz, a_oo = [
                    jnp.where(other_first, a, b) for a, b in zip(there, here)
                ]
                e_t, e_p, b_zz, b_zo, b_oz, b_oo = [
                    jnp.where(other_first, b, a) for a, b in zip(there, here)
                ]
                state = (
                    e_t + (b_zz * d_t + b_zo * d_p),
                    e_p + (b_oz * d_t + b_oo * d_p),
                    b_zz * a_zz + b_zo * a_oz,
                    b_zz * a_zo + b_zo * a_oo,
                    b_oz * a_zz + b_oo * a_oz,
                    b_oz * a_zo + b_oo * a_oo,
                )
                for k in range(6):
                    done[k, half, pl.ds(at, BLOCK), :] = state[k].reshape(BLOCK, 128)
            return carry

        lax.fori_loop(0, width // BLOCK, block, 0)

    for x in range(NX):
        pl.when(scalar_ref[0] == x)(lambda x=x: rays(x))
    for k in range(6):
        for half in range(2):
            rows = slice(half * 128, half * 128 + 128)
            turned = done[k, half].T
            if k < 2:
                disp[k, rows, :] = turned
            else:
                jac[k - 2, rows, :] = turned


def smem():
    return pl.BlockSpec(memory_space=pltpu.SMEM)


def vmem():
    return pl.BlockSpec(memory_space=pltpu.VMEM)


def ext_shape(count, rows, width):
    return (count, 2, width + 2 * PAD, rows // 2)


def fields_shape(count, rows, width):
    return (count, 2, 4, width + 2 * PAD, rows // 2)


def cost(planes, rows, width):
    return pl.CostEstimate(
        flops=260 * planes * rows * width, bytes_accessed=40 * rows * width, transcendentals=0
    )


def prepare_kernel(tile_ref, shift_ref, weight_ref, scale_ref, gain_ref, low, high, tables):
    rows, width = tile_ref.shape
    for half in range(2):
        lanes = slice(half * 128, half * 128 + 128)
        low[:, lanes] = tile_ref[lanes, width - 128 :].T[128 - HALO :]
        high[:, lanes] = tile_ref[lanes, :128].T[:HALO]
    for side, turn in ((0, rows - 1), (1, 1)):
        shift = jnp.broadcast_to(shift_ref[side : side + 1, :], (8, rows))
        frac = jnp.broadcast_to(weight_ref[side : side + 1, :].astype(jnp.float32) / 16.0, (8, rows))
        shift, frac = pltpu.roll(shift, turn, 1), pltpu.roll(frac, turn, 1)
        for tap in range(TAPS):
            value = jnp.where(shift == tap - 3, 1.0 - frac, 0.0)
            value += jnp.where(shift == tap - 4, frac, 0.0)
            for half in range(2):
                tables[side * TAPS + tap, half] = value[:, half * 128 : half * 128 + 128]
    scale = jnp.broadcast_to(scale_ref[...], (8, rows))
    for k, value in enumerate((0.5 * scale, scale * scale, 0.25 * scale)):
        for half in range(2):
            tables[2 * TAPS + k, half] = value[:, half * 128 : half * 128 + 128]
    for k in range(gain_ref.shape[1]):
        tables[2 * TAPS + 3 + k // 2, k % 2] = jnp.broadcast_to(gain_ref[:, k : k + 1], (8, rows // 2))


def prepare(tile, cycle_shift, cycle_weight, cycle_scale, lens_weight):
    rows = tile.shape[0]
    entries = 2 * TAPS + 3 + lens_weight.shape[1] // 2
    return pl.pallas_call(
        prepare_kernel,
        out_shape=(
            jax.ShapeDtypeStruct((HALO, rows), jnp.float32),
            jax.ShapeDtypeStruct((HALO, rows), jnp.float32),
            jax.ShapeDtypeStruct((entries, 2, 8, rows // 2), jnp.float32),
        ),
        in_specs=[vmem()] * 5,
        out_specs=(vmem(),) * 3,
        cost_estimate=pl.CostEstimate(flops=1 << 16, bytes_accessed=1 << 20, transcendentals=0),
        name="prepare",
    )(tile, cycle_shift, cycle_weight, cycle_scale[None], lens_weight)


def per_device(potential, lens_weight, cycle_shift, cycle_weight, cycle_scale):
    tile = potential[0]
    rows, width = tile.shape
    lon, plane = lax.axis_index("lon"), lax.axis_index("plane")
    near_hi = (((plane // NX) * Z_LO + lon // RING + 1) // Z_LO) % Z_HI
    scalars = jnp.where(jnp.arange(2) == 0, plane % NX, near_hi).astype(jnp.int32)

    near, far = z_move(tile, 1), z_move(tile, 1 + Z_LO)
    low, high, tables = prepare(tile, cycle_shift, cycle_weight, cycle_scale, lens_weight)
    strips = jnp.concatenate([z_move(low, 1, -1), z_move(high, 1, 1)])
    near = jnp.concatenate([near, strips])
    near_tiles = [near] + [x_move(near, ahead) for ahead in NEAR[1:]]
    far = jnp.concatenate([far, swap(strips)])
    far_tiles = [far] + [x_move(far, ahead) for ahead in FAR[1:]]

    params = pltpu.CompilerParams(vmem_limit_bytes=24 << 20)
    state_shape = (6, 2, width, rows // 2)
    state = pl.pallas_call(
        near_kernel,
        out_shape=jax.ShapeDtypeStruct(state_shape, jnp.float32),
        in_specs=[smem()] + [vmem()] * 5,
        out_specs=vmem(),
        scratch_shapes=[
            pltpu.VMEM(ext_shape(NX, rows, width), jnp.float32),
            pltpu.VMEM(fields_shape(NX, rows, width), jnp.float32),
        ],
        cost_estimate=cost(NX, rows, width),
        compiler_params=params,
        name="near_planes",
    )(scalars, tables, *near_tiles)
    early = pl.pallas_call(
        early_kernel,
        out_shape=jax.ShapeDtypeStruct(fields_shape(NX - 1, rows, width), jnp.float32),
        in_specs=[vmem()] * NX + [pl.BlockSpec(memory_space=pl.ANY)],
        out_specs=vmem(),
        scratch_shapes=[pltpu.VMEM(ext_shape(NX - 1, rows, width), jnp.float32)],
        cost_estimate=cost(NX // 2, rows, width),
        compiler_params=params,
        name="far_planes_early",
    )(tables, *far_tiles[: NX - 1], state)
    displacement, jacobian = pl.pallas_call(
        far_kernel,
        out_shape=(
            jax.ShapeDtypeStruct((2, rows, width), jnp.float32),
            jax.ShapeDtypeStruct((4, rows, width), jnp.float32),
        ),
        in_specs=[smem()] + [vmem()] * 4,
        out_specs=(vmem(), vmem()),
        scratch_shapes=[
            pltpu.VMEM(ext_shape(1, rows, width), jnp.float32),
            pltpu.VMEM(fields_shape(1, rows, width), jnp.float32),
            pltpu.VMEM(state_shape, jnp.float32),
        ],
        cost_estimate=cost(NX, rows, width),
        compiler_params=params,
        name="far_planes",
    )(scalars, tables, far_tiles[NX - 1], early, state)
    return displacement[None], jacobian[None]


def solution(mesh):
    in_specs = (P("plane", None, "lon"), P("plane", None), P(), P(), P())
    out_specs = (P("plane", None, None, "lon"), P("plane", None, None, "lon"))
    return jax.shard_map(
        per_device, mesh=mesh, in_specs=in_specs, out_specs=out_specs, check_vma=False
    )
```

time: 69.2 us -> 68.2 us (0.986)
  other arithmetic: 0.77 us -> 0.03 us
  local copies, waits for them, and re-layouts: 1.66 us -> 0.94 us
  waiting for transfers between devices: 9.69 us -> 10.4 us
    concatenate x1 -> x0, other arithmetic: 0.73 us -> none  [per_device(): scalars = jnp.concatenate([places, lens_weight[0]])]
    ppermute x6, waiting for transfers between devices: 4.08 us -> 4.81 us  [x_move(): return lax.ppermute(value, 'plane', pairs)]
    unnamed x5 -> x3, local copies, waits for them, and re-layouts: 1.65 us -> 0.94 us
    pallas_call x2 -> x3, Pallas kernels: 9.82 us -> 9.54 us  [the longest x1 4.24 us: per_device(): pl.pallas_call(far_kernel, out_shape=(jax.ShapeDtypeStruct((2, rows, widt...]
  transfers between devices with their start and end apart: 11 -> 11, of which waited for: 2 -> 2; matrix products, arithmetic and copies ran while one was open for 1% -> 0% of each run, Pallas kernels for 9% -> 11%
where the time goes in v3:
time: 68.2 us; the launch traced here: 67.7 us
  starting transfers between devices  44 us (65%)
  Pallas kernels  11.4 us (17%)
  waiting for transfers between devices  10.4 us (15%)
  local copies, waits for them, and re-layouts  0.94 us (1%)
  between operations  0.9 us (1%)
    ppermute x4, starting transfers between devices, z_move(): return lax.ppermute(value, ('lon', 'plane'), pairs)  19.7 us
    ppermute x6, starting transfers between devices, x_move(): return lax.ppermute(value, 'plane', pairs)  17.7 us
    ppermute x1, starting transfers between devices, swap(): return lax.ppermute(value, 'plane', pairs)  6.64 us
    ppermute x4, waiting for transfers between devices, z_move(): return lax.ppermute(value, ('lon', 'plane'), pairs)  5.61 us
    ppermute x6, waiting for transfers between devices, x_move(): return lax.ppermute(value, 'plane', pairs)  4.81 us
    pallas_call x1, Pallas kernels, per_device(): pl.pallas_call(far_kernel, out_shape=(jax.ShapeDtypeStruct((2, rows, widt...  4.24 us
    pallas_call x1, Pallas kernels, per_device(): pl.pallas_call(near_kernel, out_shape=jax.ShapeDtypeStruct(state_shape, j...  3.68 us
    pallas_call x1, Pallas kernels, prepare(): pl.pallas_call(prepare_kernel, out_shape=(jax.ShapeDtypeStruct((HALO, row...  1.85 us
  transfers between devices with their start and end apart: 11, of which 2 were waited for; matrix products, arithmetic and copies ran while one was open for 0% of the time, Pallas kernels for 11%

profile of v3, /device:TPU:31, one launch (start us, length us, event | category | flops | bytes accessed | tf_op | source)
XLA Modules:
  0.0 67.7 jit_solution(9046219047491119764)
XLA Ops:
  0.6 10.7 %collective-permute-start.7 = (f32[256,256]{1,0:T(8,128)}, f32[256,256]{1,0:T(8,128)S(1)}, u32[]{:S(2)}, u32[]{:S(2)}) collective-permute-start(f32[256,256]{1,0:T(8,128)} %bitcast.4), channel_id=1, source_target_pairs={{128,0},{129,1},{130,2},{131,3},{136,8},{137,9},{138,10},{139,11},... | collective-permute-start | bytes 786440 | tf_op jit(solution)/shard_map/ppermute | solution.py:29
  11.3 1.9 %collective-permute-start = (f32[256,256]{1,0:T(8,128)}, f32[256,256]{1,0:T(8,128)S(1)}, u32[]{:S(2)}, u32[]{:S(2)}) collective-permute-start(f32[256,256]{1,0:T(8,128)} %bitcast.5), channel_id=1, source_target_pairs={{132,0},{133,1},{134,2},{135,3},{140,8},{141,9},{142,10},{143,11},... | collective-permute-start | bytes 786440 | tf_op jit(solution)/shard_map/ppermute | solution.py:29
  13.2 1.8 %prepare.1 = (f32[4,256]{1,0:T(4,128)}, f32[4,256]{1,0:T(4,128)}, f32[21,2,8,128]{3,2,1,0:T(8,128)}) custom-call(f32[256,256]{1,0:T(8,128)} %bitcast.6, s32[2,256]{1,0:T(2,128)} %shift_ref.1, s32[2,256]{1,0:T(2,128)} %weight_ref.1, f32[1,256]{1,0:T(1,128)} %bitcast.7, f32[1,8]{1,0:T(1,128)} %gain_ref.1), custom_call_target="tpu_custom_call" | custom-call | flops 65536 | bytes 1048576 | tf_op jit(solution)/shard_map/prepare/pallas_call | solution.py:249
  15.1 5.2 %collective-permute-start.1 = (f32[4,256]{1,0:T(4,128)}, f32[4,256]{1,0:T(4,128)S(1)}, u32[]{:S(2)}, u32[]{:S(2)}) collective-permute-start(f32[4,256]{1,0:T(4,128)} %get-tuple-element.8), channel_id=1, source_target_pairs={{120,0},{121,1},{122,2},{123,3},{128,8},{129,9},{130,10},{131,11},... | collective-permute-start | bytes 12296 | tf_op jit(solution)/shard_map/ppermute | solution.py:29
  20.3 1.9 %collective-permute-start.2 = (f32[4,256]{1,0:T(4,128)}, f32[4,256]{1,0:T(4,128)S(1)}, u32[]{:S(2)}, u32[]{:S(2)}) collective-permute-start(f32[4,256]{1,0:T(4,128)} %get-tuple-element.9), channel_id=1, source_target_pairs={{136,0},{137,1},{138,2},{139,3},{144,8},{145,9},{146,10},{147,11},... | collective-permute-start | bytes 12296 | tf_op jit(solution)/shard_map/ppermute | solution.py:29
  22.3 0.0 collective-permute-done.1
  22.3 5.6 %collective-permute-done.2 = f32[4,256]{1,0:T(4,128)S(1)} collective-permute-done((f32[4,256]{1,0:T(4,128)}, f32[4,256]{1,0:T(4,128)S(1)}, u32[]{:S(2)}, u32[]{:S(2)}) %collective-permute-start.2) | collective-permute-done | bytes 4128 | tf_op jit(solution)/shard_map/ppermute | solution.py:29
  27.9 0.0 collective-permute-done.7
  27.9 3.0 %collective-permute-start.10 = (f32[264,256]{1,0:T(8,128)S(1)}, f32[264,256]{1,0:T(8,128)S(1)}, u32[]{:S(2)}, u32[]{:S(2)}) collective-permute-start(f32[264,256]{1,0:T(8,128)S(1)} %pad_maximum_fusion.t0), channel_id=1, source_target_pairs={{2,0},{3,1},{0,2},{1,3},{6,4},{7,5},{4,6},{5,7},{10,8},{11,9},{8,1... | collective-permute-start | bytes 811016 | tf_op jit(solution)/shard_map/ppermute | solution.py:41
  30.9 6.6 %collective-permute-start.3 = (f32[8,256]{1,0:T(8,128)S(1)}, f32[8,256]{1,0:T(8,128)S(1)}, u32[]{:S(2)}, u32[]{:S(2)}) collective-permute-start(f32[8,256]{1,0:T(8,128)S(1)} %pad_maximum_fusion.1), channel_id=1, source_target_pairs={{0,4},{1,5},{2,6},{3,7},{4,0},{5,1},{6,2},{7,3},{8,12},{9,13},{10,... | collective-permute-start | bytes 24584 | tf_op jit(solution)/shard_map/ppermute | solution.py:34
  37.6 3.7 %collective-permute-start.9 = (f32[264,256]{1,0:T(8,128)S(1)}, f32[264,256]{1,0:T(8,128)S(1)}, u32[]{:S(2)}, u32[]{:S(2)}) collective-permute-start(f32[264,256]{1,0:T(8,128)S(1)} %pad_maximum_fusion.t0), channel_id=1, source_target_pairs={{3,0},{0,1},{1,2},{2,3},{7,4},{4,5},{5,6},{6,7},{11,8},{8,9},{9,10... | collective-permute-start | bytes 811016 | tf_op jit(solution)/shard_map/ppermute | solution.py:41
  41.3 1.9 %collective-permute-start.8 = (f32[264,256]{1,0:T(8,128)S(1)}, f32[264,256]{1,0:T(8,128)S(1)}, u32[]{:S(2)}, u32[]{:S(2)}) collective-permute-start(f32[264,256]{1,0:T(8,128)S(1)} %pad_maximum_fusion.t0), channel_id=1, source_target_pairs={{1,0},{2,1},{3,2},{0,3},{5,4},{6,5},{7,6},{4,7},{9,8},{10,9},{11,1... | collective-permute-start | bytes 811016 | tf_op jit(solution)/shard_map/ppermute | solution.py:41
  43.3 0.0 collective-permute-done
  43.3 0.0 collective-permute-done.3
  43.3 3.4 %collective-permute-start.6 = (f32[264,256]{1,0:T(8,128)S(1)}, f32[264,256]{1,0:T(8,128)S(1)}, u32[]{:S(2)}, u32[]{:S(2)}) collective-permute-start(f32[264,256]{1,0:T(8,128)S(1)} %constant_dynamic-update-slice_fusion.t0), channel_id=1, source_target_pairs={{2,0},{3,1},{0,2},{1,3},{6,4},{7,5},{4,6},{5,7},{10,8},{11,9},{8,1... | collective-permute-start | bytes 811016 | tf_op jit(solution)/shard_map/ppermute | solution.py:41
  46.7 3.1 %collective-permute-start.5 = (f32[264,256]{1,0:T(8,128)S(1)}, f32[264,256]{1,0:T(8,128)S(1)}, u32[]{:S(2)}, u32[]{:S(2)}) collective-permute-start(f32[264,256]{1,0:T(8,128)S(1)} %constant_dynamic-update-slice_fusion.t0), channel_id=1, source_target_pairs={{3,0},{0,1},{1,2},{2,3},{7,4},{4,5},{5,6},{6,7},{11,8},{8,9},{9,10... | collective-permute-start | bytes 811016 | tf_op jit(solution)/shard_map/ppermute | solution.py:41
  49.8 0.0 collective-permute-done.10.t3
  49.8 2.5 %collective-permute-start.4 = (f32[264,256]{1,0:T(8,128)S(1)}, f32[264,256]{1,0:T(8,128)S(1)}, u32[]{:S(2)}, u32[]{:S(2)}) collective-permute-start(f32[264,256]{1,0:T(8,128)S(1)} %constant_dynamic-update-slice_fusion.t0), channel_id=1, source_target_pairs={{1,0},{2,1},{3,2},{0,3},{5,4},{6,5},{7,6},{4,7},{9,8},{10,9},{11,1... | collective-permute-start | bytes 811016 | tf_op jit(solution)/shard_map/ppermute | solution.py:41
  52.4 0.0 collective-permute-done.9.t2
  52.4 4.8 %collective-permute-done.8.t1 = f32[264,256]{1,0:T(8,128)S(1)} collective-permute-done((f32[264,256]{1,0:T(8,128)S(1)}, f32[264,256]{1,0:T(8,128)S(1)}, u32[]{:S(2)}, u32[]{:S(2)}) %collective-permute-start.8) | collective-permute-done | bytes 270368 | tf_op jit(solution)/shard_map/ppermute | solution.py:41
  57.2 0.0 copy-start
  57.2 0.9 %copy-done = f32[21,2,8,128]{3,2,1,0:T(8,128)S(1)} copy-done((f32[21,2,8,128]{3,2,1,0:T(8,128)S(1)}, f32[21,2,8,128]{3,2,1,0:T(8,128)}, u32[]{:S(2)}) %copy-start) | copy-done | bytes 172056
  58.1 3.7 %near_planes.1.after.other = f32[6,2,256,128]{3,2,1,0:T(8,128)S(1)} custom-call(s32[2]{0:T(128)S(1)} %compare_select_fusion.scalar_ref, f32[21,2,8,128]{3,2,1,0:T(8,128)S(1)} %copy-done, f32[264,256]{1,0:T(8,128)S(1)} %pad_maximum_fusion.t0, f32[264,256]{1,0:T(8,128)S(1)} %collective-permute-done.8.t1, f32[264,256]{1,0:T(8,128)S(1)} %collective-permute-done.9.t2, ...), custom_call_target="tpu_custom_call" | custom-call | flops 68157440 | bytes 2621440 | tf_op jit(solution)/shard_map/near_planes/pallas_call | solution.py:280
  61.8 0.0 collective-permute-done.6.t2
  61.8 0.0 collective-permute-done.5.t1
  61.9 1.6 %far_planes_early.1.early = f32[3,2,4,304,128]{4,3,2,1,0:T(8,128)S(1)} custom-call(f32[21,2,8,128]{3,2,1,0:T(8,128)S(1)} %copy-done, f32[264,256]{1,0:T(8,128)S(1)} %constant_dynamic-update-slice_fusion.t0, f32[264,256]{1,0:T(8,128)S(1)} %collective-permute-done.5.t1, f32[264,256]{1,0:T(8,128)S(1)} %collective-permute-done.6.t2, ...), custom_call_target="tpu_custom_call" | custom-call | flops 34078720 | bytes 2621440 | tf_op jit(solution)/shard_map/far_planes_early/pallas_call | solution.py:293
  63.5 0.0 collective-permute-done.4.last
  63.5 4.2 %far_planes.1 = (f32[2,256,256]{2,1,0:T(8,128)}, f32[4,256,256]{2,1,0:T(8,128)}) custom-call(s32[2]{0:T(128)S(1)} %compare_select_fusion.scalar_ref, f32[21,2,8,128]{3,2,1,0:T(8,128)S(1)} %copy-done, f32[264,256]{1,0:T(8,128)S(1)} %collective-permute-done.4.last, f32[3,2,4,304,128]{4,3,2,1,0:T(8,128)S(1)} %far_planes_early.1.early, ...), custom_call_target="tpu_custom_call" | custom-call | flops 68157440 | bytes 2621440 | tf_op jit(solution)/shard_map/far_planes/pallas_call | solution.py:303
  (5 shorter events, 0.1 us)
Async XLA Ops:
  0.6 27.2 %collective-permute-start.7 = (f32[256,256]{1,0:T(8,128)}, f32[256,256]{1,0:T(8,128)S(1)}, u32[]{:S(2)}, u32[]{:S(2)}) collective-permute-start(f32[256,256]{1,0:T(8,128)} %bitcast.4), channel_id=1, source_target_pairs={{128,0},{129,1},{130,2},{131,3},{136,8},{137,9},{138,10},{139,11},... | collective-permute-start | bytes 786440 | tf_op jit(solution)/shard_map/ppermute | solution.py:29
  11.3 32.0 %collective-permute-start = (f32[256,256]{1,0:T(8,128)}, f32[256,256]{1,0:T(8,128)S(1)}, u32[]{:S(2)}, u32[]{:S(2)}) collective-permute-start(f32[256,256]{1,0:T(8,128)} %bitcast.5), channel_id=1, source_target_pairs={{132,0},{133,1},{134,2},{135,3},{140,8},{141,9},{142,10},{143,11},... | collective-permute-start | bytes 786440 | tf_op jit(solution)/shard_map/ppermute | solution.py:29
  15.1 7.2 %collective-permute-start.1 = (f32[4,256]{1,0:T(4,128)}, f32[4,256]{1,0:T(4,128)S(1)}, u32[]{:S(2)}, u32[]{:S(2)}) collective-permute-start(f32[4,256]{1,0:T(4,128)} %get-tuple-element.8), channel_id=1, source_target_pairs={{120,0},{121,1},{122,2},{123,3},{128,8},{129,9},{130,10},{131,11},... | collective-permute-start | bytes 12296 | tf_op jit(solution)/shard_map/ppermute | solution.py:29
  20.3 7.5 %collective-permute-start.2 = (f32[4,256]{1,0:T(4,128)}, f32[4,256]{1,0:T(4,128)S(1)}, u32[]{:S(2)}, u32[]{:S(2)}) collective-permute-start(f32[4,256]{1,0:T(4,128)} %get-tuple-element.9), channel_id=1, source_target_pairs={{136,0},{137,1},{138,2},{139,3},{144,8},{145,9},{146,10},{147,11},... | collective-permute-start | bytes 12296 | tf_op jit(solution)/shard_map/ppermute | solution.py:29
  27.9 21.9 %collective-permute-start.10 = (f32[264,256]{1,0:T(8,128)S(1)}, f32[264,256]{1,0:T(8,128)S(1)}, u32[]{:S(2)}, u32[]{:S(2)}) collective-permute-start(f32[264,256]{1,0:T(8,128)S(1)} %pad_maximum_fusion.t0), channel_id=1, source_target_pairs={{2,0},{3,1},{0,2},{1,3},{6,4},{7,5},{4,6},{5,7},{10,8},{11,9},{8,1... | collective-permute-start | bytes 811016 | tf_op jit(solution)/shard_map/ppermute | solution.py:41
  30.9 12.3 %collective-permute-start.3 = (f32[8,256]{1,0:T(8,128)S(1)}, f32[8,256]{1,0:T(8,128)S(1)}, u32[]{:S(2)}, u32[]{:S(2)}) collective-permute-start(f32[8,256]{1,0:T(8,128)S(1)} %pad_maximum_fusion.1), channel_id=1, source_target_pairs={{0,4},{1,5},{2,6},{3,7},{4,0},{5,1},{6,2},{7,3},{8,12},{9,13},{10,... | collective-permute-start | bytes 24584 | tf_op jit(solution)/shard_map/ppermute | solution.py:34
  37.6 14.8 %collective-permute-start.9 = (f32[264,256]{1,0:T(8,128)S(1)}, f32[264,256]{1,0:T(8,128)S(1)}, u32[]{:S(2)}, u32[]{:S(2)}) collective-permute-start(f32[264,256]{1,0:T(8,128)S(1)} %pad_maximum_fusion.t0), channel_id=1, source_target_pairs={{3,0},{0,1},{1,2},{2,3},{7,4},{4,5},{5,6},{6,7},{11,8},{8,9},{9,10... | collective-permute-start | bytes 811016 | tf_op jit(solution)/shard_map/ppermute | solution.py:41
  41.3 15.9 %collective-permute-start.8 = (f32[264,256]{1,0:T(8,128)S(1)}, f32[264,256]{1,0:T(8,128)S(1)}, u32[]{:S(2)}, u32[]{:S(2)}) collective-permute-start(f32[264,256]{1,0:T(8,128)S(1)} %pad_maximum_fusion.t0), channel_id=1, source_target_pairs={{1,0},{2,1},{3,2},{0,3},{5,4},{6,5},{7,6},{4,7},{9,8},{10,9},{11,1... | collective-permute-start | bytes 811016 | tf_op jit(solution)/shard_map/ppermute | solution.py:41
  43.3 18.5 %collective-permute-start.6 = (f32[264,256]{1,0:T(8,128)S(1)}, f32[264,256]{1,0:T(8,128)S(1)}, u32[]{:S(2)}, u32[]{:S(2)}) collective-permute-start(f32[264,256]{1,0:T(8,128)S(1)} %constant_dynamic-update-slice_fusion.t0), channel_id=1, source_target_pairs={{2,0},{3,1},{0,2},{1,3},{6,4},{7,5},{4,6},{5,7},{10,8},{11,9},{8,1... | collective-permute-start | bytes 811016 | tf_op jit(solution)/shard_map/ppermute | solution.py:41
  46.7 15.1 %collective-permute-start.5 = (f32[264,256]{1,0:T(8,128)S(1)}, f32[264,256]{1,0:T(8,128)S(1)}, u32[]{:S(2)}, u32[]{:S(2)}) collective-permute-start(f32[264,256]{1,0:T(8,128)S(1)} %constant_dynamic-update-slice_fusion.t0), channel_id=1, source_target_pairs={{3,0},{0,1},{1,2},{2,3},{7,4},{4,5},{5,6},{6,7},{11,8},{8,9},{9,10... | collective-permute-start | bytes 811016 | tf_op jit(solution)/shard_map/ppermute | solution.py:41
  49.8 13.6 %collective-permute-start.4 = (f32[264,256]{1,0:T(8,128)S(1)}, f32[264,256]{1,0:T(8,128)S(1)}, u32[]{:S(2)}, u32[]{:S(2)}) collective-permute-start(f32[264,256]{1,0:T(8,128)S(1)} %constant_dynamic-update-slice_fusion.t0), channel_id=1, source_target_pairs={{1,0},{2,1},{3,2},{0,3},{5,4},{6,5},{7,6},{4,7},{9,8},{10,9},{11,1... | collective-permute-start | bytes 811016 | tf_op jit(solution)/shard_map/ppermute | solution.py:41
  57.2 0.9 %copy-start = (f32[21,2,8,128]{3,2,1,0:T(8,128)S(1)}, f32[21,2,8,128]{3,2,1,0:T(8,128)}, u32[]{:S(2)}) copy-start(f32[21,2,8,128]{3,2,1,0:T(8,128)} %get-tuple-element.7.tables) | copy-start | bytes 516100

commit v4 on v3

--- a/solution.py
+++ b/solution.py
@@ -147,14 +147,16 @@
     stencils(t0.shape[1], tables, ext, fields)
 
 
-def far_kernel(scalar_ref, tables, last, early, other, disp, jac, ext, fields, done):
+def far_kernel(
+    scalar_ref, tables, last, early, other, disp, jac, ext, fields, done, stage, sems
+):
     width = last.shape[1]
     load_planes(range(1), (last,), ext)
     stencils(width, tables, ext, fields)
     hi = 1 - scalar_ref[1]
     other_first = hi == 1
 
-    def rays(x):
+    def rays(x, part):
         def block(j, carry):
             at = pl.multiple_of(j * BLOCK, BLOCK)
             for half in range(2):
@@ -184,18 +186,26 @@
                     done[k, half, pl.ds(at, BLOCK), :] = state[k].reshape(BLOCK, 128)
             return carry
 
-        lax.fori_loop(0, width // BLOCK, block, 0)
-
-    for x in range(NX):
-        pl.when(scalar_ref[0] == x)(lambda x=x: rays(x))
-    for k in range(6):
-        for half in range(2):
-            rows = slice(half * 128, half * 128 + 128)
-            turned = done[k, half].T
-            if k < 2:
-                disp[k, rows, :] = turned
-            else:
-                jac[k - 2, rows, :] = turned
+        count = width // BLOCK // 2
+        lax.fori_loop(part * count, part * count + count, block, 0)
+
+    copies = []
+    for part in range(2):
+        for x in range(NX):
+            pl.when(scalar_ref[0] == x)(lambda x=x, part=part: rays(x, part))
+        columns = slice(part * 128, part * 128 + 128)
+        for k in range(6):
+            for half in range(2):
+                rows = slice(half * 128, half * 128 + 128)
+                stage[k, rows, columns] = done[k, half, columns].T
+            target = disp.at[k] if k < 2 else jac.at[k - 2]
+            copy = pltpu.make_async_copy(
+                stage.at[k, :, columns], target.at[:, columns], sems.at[part * 6 + k]
+            )
+            copy.start()
+            copies.append(copy)
+    for copy in copies:
+        copy.wait()
 
 
 def smem():
@@ -307,11 +317,13 @@
             jax.ShapeDtypeStruct((4, rows, width), jnp.float32),
         ),
         in_specs=[smem()] + [vmem()] * 4,
-        out_specs=(vmem(), vmem()),
+        out_specs=(pl.BlockSpec(memory_space=pl.ANY),) * 2,
         scratch_shapes=[
             pltpu.VMEM(ext_shape(1, rows, width), jnp.float32),
             pltpu.VMEM(fields_shape(1, rows, width), jnp.float32),
             pltpu.VMEM(state_shape, jnp.float32),
+            pltpu.VMEM((6, rows, width), jnp.float32),
+            pltpu.SemaphoreType.DMA((12,)),
         ],
         cost_estimate=cost(NX, rows, width),
         compiler_params=params,

time: 68.2 us -> 68.1 us (level)
  no operation moved by 1% of the time
where the time goes in v4:
time: 68.1 us; the launch traced here: 67.6 us
  starting transfers between devices  44 us (65%)
  Pallas kernels  11.3 us (17%)
  waiting for transfers between devices  10.4 us (15%)
  local copies, waits for them, and re-layouts  0.94 us (1%)
  between operations  0.9 us (1%)
    ppermute x4, starting transfers between devices, z_move(): return lax.ppermute(value, ('lon', 'plane'), pairs)  19.7 us
    ppermute x6, starting transfers between devices, x_move(): return lax.ppermute(value, 'plane', pairs)  17.7 us
    ppermute x1, starting transfers between devices, swap(): return lax.ppermute(value, 'plane', pairs)  6.64 us
    ppermute x4, waiting for transfers between devices, z_move(): return lax.ppermute(value, ('lon', 'plane'), pairs)  5.61 us
    ppermute x6, waiting for transfers between devices, x_move(): return lax.ppermute(value, 'plane', pairs)  4.81 us
    pallas_call x1, Pallas kernels, per_device(): pl.pallas_call(far_kernel, out_shape=(jax.ShapeDtypeStruct((2, rows, widt...  4.15 us
    pallas_call x1, Pallas kernels, per_device(): pl.pallas_call(near_kernel, out_shape=jax.ShapeDtypeStruct(state_shape, j...  3.68 us
    pallas_call x1, Pallas kernels, prepare(): pl.pallas_call(prepare_kernel, out_shape=(jax.ShapeDtypeStruct((HALO, row...  1.85 us
  transfers between devices with their start and end apart: 11, of which 2 were waited for; matrix products, arithmetic and copies ran while one was open for 0% of the time, Pallas kernels for 11%

profile of v4, /device:TPU:31, one launch (start us, length us, event | category | flops | bytes accessed | tf_op | source)
XLA Modules:
  0.0 67.6 jit_solution(14762644915350424498)
XLA Ops:
  0.6 10.7 %collective-permute-start.7 = (f32[256,256]{1,0:T(8,128)}, f32[256,256]{1,0:T(8,128)S(1)}, u32[]{:S(2)}, u32[]{:S(2)}) collective-permute-start(f32[256,256]{1,0:T(8,128)} %bitcast.4), channel_id=1, source_target_pairs={{128,0},{129,1},{130,2},{131,3},{136,8},{137,9},{138,10},{139,11},... | collective-permute-start | bytes 786440 | tf_op jit(solution)/shard_map/ppermute | solution.py:29
  11.3 1.9 %collective-permute-start = (f32[256,256]{1,0:T(8,128)}, f32[256,256]{1,0:T(8,128)S(1)}, u32[]{:S(2)}, u32[]{:S(2)}) collective-permute-start(f32[256,256]{1,0:T(8,128)} %bitcast.5), channel_id=1, source_target_pairs={{132,0},{133,1},{134,2},{135,3},{140,8},{141,9},{142,10},{143,11},... | collective-permute-start | bytes 786440 | tf_op jit(solution)/shard_map/ppermute | solution.py:29
  13.2 1.8 %prepare.1 = (f32[4,256]{1,0:T(4,128)}, f32[4,256]{1,0:T(4,128)}, f32[21,2,8,128]{3,2,1,0:T(8,128)}) custom-call(f32[256,256]{1,0:T(8,128)} %bitcast.6, s32[2,256]{1,0:T(2,128)} %shift_ref.1, s32[2,256]{1,0:T(2,128)} %weight_ref.1, f32[1,256]{1,0:T(1,128)} %bitcast.7, f32[1,8]{1,0:T(1,128)} %gain_ref.1), custom_call_target="tpu_custom_call" | custom-call | flops 65536 | bytes 1048576 | tf_op jit(solution)/shard_map/prepare/pallas_call | solution.py:259
  15.1 5.2 %collective-permute-start.1 = (f32[4,256]{1,0:T(4,128)}, f32[4,256]{1,0:T(4,128)S(1)}, u32[]{:S(2)}, u32[]{:S(2)}) collective-permute-start(f32[4,256]{1,0:T(4,128)} %get-tuple-element.8), channel_id=1, source_target_pairs={{120,0},{121,1},{122,2},{123,3},{128,8},{129,9},{130,10},{131,11},... | collective-permute-start | bytes 12296 | tf_op jit(solution)/shard_map/ppermute | solution.py:29
  20.3 1.9 %collective-permute-start.2 = (f32[4,256]{1,0:T(4,128)}, f32[4,256]{1,0:T(4,128)S(1)}, u32[]{:S(2)}, u32[]{:S(2)}) collective-permute-start(f32[4,256]{1,0:T(4,128)} %get-tuple-element.9), channel_id=1, source_target_pairs={{136,0},{137,1},{138,2},{139,3},{144,8},{145,9},{146,10},{147,11},... | collective-permute-start | bytes 12296 | tf_op jit(solution)/shard_map/ppermute | solution.py:29
  22.3 0.0 collective-permute-done.1
  22.3 5.6 %collective-permute-done.2 = f32[4,256]{1,0:T(4,128)S(1)} collective-permute-done((f32[4,256]{1,0:T(4,128)}, f32[4,256]{1,0:T(4,128)S(1)}, u32[]{:S(2)}, u32[]{:S(2)}) %collective-permute-start.2) | collective-permute-done | bytes 4128 | tf_op jit(solution)/shard_map/ppermute | solution.py:29
  27.9 0.0 collective-permute-done.7
  27.9 3.0 %collective-permute-start.10 = (f32[264,256]{1,0:T(8,128)S(1)}, f32[264,256]{1,0:T(8,128)S(1)}, u32[]{:S(2)}, u32[]{:S(2)}) collective-permute-start(f32[264,256]{1,0:T(8,128)S(1)} %pad_maximum_fusion.t0), channel_id=1, source_target_pairs={{2,0},{3,1},{0,2},{1,3},{6,4},{7,5},{4,6},{5,7},{10,8},{11,9},{8,1... | collective-permute-start | bytes 811016 | tf_op jit(solution)/shard_map/ppermute | solution.py:41
  30.9 6.6 %collective-permute-start.3 = (f32[8,256]{1,0:T(8,128)S(1)}, f32[8,256]{1,0:T(8,128)S(1)}, u32[]{:S(2)}, u32[]{:S(2)}) collective-permute-start(f32[8,256]{1,0:T(8,128)S(1)} %pad_maximum_fusion.1), channel_id=1, source_target_pairs={{0,4},{1,5},{2,6},{3,7},{4,0},{5,1},{6,2},{7,3},{8,12},{9,13},{10,... | collective-permute-start | bytes 24584 | tf_op jit(solution)/shard_map/ppermute | solution.py:34
  37.6 3.7 %collective-permute-start.9 = (f32[264,256]{1,0:T(8,128)S(1)}, f32[264,256]{1,0:T(8,128)S(1)}, u32[]{:S(2)}, u32[]{:S(2)}) collective-permute-start(f32[264,256]{1,0:T(8,128)S(1)} %pad_maximum_fusion.t0), channel_id=1, source_target_pairs={{3,0},{0,1},{1,2},{2,3},{7,4},{4,5},{5,6},{6,7},{11,8},{8,9},{9,10... | collective-permute-start | bytes 811016 | tf_op jit(solution)/shard_map/ppermute | solution.py:41
  41.3 1.9 %collective-permute-start.8 = (f32[264,256]{1,0:T(8,128)S(1)}, f32[264,256]{1,0:T(8,128)S(1)}, u32[]{:S(2)}, u32[]{:S(2)}) collective-permute-start(f32[264,256]{1,0:T(8,128)S(1)} %pad_maximum_fusion.t0), channel_id=1, source_target_pairs={{1,0},{2,1},{3,2},{0,3},{5,4},{6,5},{7,6},{4,7},{9,8},{10,9},{11,1... | collective-permute-start | bytes 811016 | tf_op jit(solution)/shard_map/ppermute | solution.py:41
  43.3 0.0 collective-permute-done
  43.3 0.0 collective-permute-done.3
  43.3 3.4 %collective-permute-start.6 = (f32[264,256]{1,0:T(8,128)S(1)}, f32[264,256]{1,0:T(8,128)S(1)}, u32[]{:S(2)}, u32[]{:S(2)}) collective-permute-start(f32[264,256]{1,0:T(8,128)S(1)} %constant_dynamic-update-slice_fusion.t0), channel_id=1, source_target_pairs={{2,0},{3,1},{0,2},{1,3},{6,4},{7,5},{4,6},{5,7},{10,8},{11,9},{8,1... | collective-permute-start | bytes 811016 | tf_op jit(solution)/shard_map/ppermute | solution.py:41
  46.7 3.1 %collective-permute-start.5 = (f32[264,256]{1,0:T(8,128)S(1)}, f32[264,256]{1,0:T(8,128)S(1)}, u32[]{:S(2)}, u32[]{:S(2)}) collective-permute-start(f32[264,256]{1,0:T(8,128)S(1)} %constant_dynamic-update-slice_fusion.t0), channel_id=1, source_target_pairs={{3,0},{0,1},{1,2},{2,3},{7,4},{4,5},{5,6},{6,7},{11,8},{8,9},{9,10... | collective-permute-start | bytes 811016 | tf_op jit(solution)/shard_map/ppermute | solution.py:41
  49.8 0.0 collective-permute-done.10.t3
  49.8 2.5 %collective-permute-start.4 = (f32[264,256]{1,0:T(8,128)S(1)}, f32[264,256]{1,0:T(8,128)S(1)}, u32[]{:S(2)}, u32[]{:S(2)}) collective-permute-start(f32[264,256]{1,0:T(8,128)S(1)} %constant_dynamic-update-slice_fusion.t0), channel_id=1, source_target_pairs={{1,0},{2,1},{3,2},{0,3},{5,4},{6,5},{7,6},{4,7},{9,8},{10,9},{11,1... | collective-permute-start | bytes 811016 | tf_op jit(solution)/shard_map/ppermute | solution.py:41
  52.4 0.0 collective-permute-done.9.t2
  52.4 4.8 %collective-permute-done.8.t1 = f32[264,256]{1,0:T(8,128)S(1)} collective-permute-done((f32[264,256]{1,0:T(8,128)S(1)}, f32[264,256]{1,0:T(8,128)S(1)}, u32[]{:S(2)}, u32[]{:S(2)}) %collective-permute-start.8) | collective-permute-done | bytes 270368 | tf_op jit(solution)/shard_map/ppermute | solution.py:41
  57.2 0.0 copy-start
  57.2 0.9 %copy-done = f32[21,2,8,128]{3,2,1,0:T(8,128)S(1)} copy-done((f32[21,2,8,128]{3,2,1,0:T(8,128)S(1)}, f32[21,2,8,128]{3,2,1,0:T(8,128)}, u32[]{:S(2)}) %copy-start) | copy-done | bytes 172056
  58.1 3.7 %near_planes.1.after.other = f32[6,2,256,128]{3,2,1,0:T(8,128)S(1)} custom-call(s32[2]{0:T(128)S(1)} %compare_select_fusion.scalar_ref, f32[21,2,8,128]{3,2,1,0:T(8,128)S(1)} %copy-done, f32[264,256]{1,0:T(8,128)S(1)} %pad_maximum_fusion.t0, f32[264,256]{1,0:T(8,128)S(1)} %collective-permute-done.8.t1, f32[264,256]{1,0:T(8,128)S(1)} %collective-permute-done.9.t2, ...), custom_call_target="tpu_custom_call" | custom-call | flops 68157440 | bytes 2621440 | tf_op jit(solution)/shard_map/near_planes/pallas_call | solution.py:290
  61.8 0.0 collective-permute-done.6.t2
  61.8 0.0 collective-permute-done.5.t1
  61.9 1.6 %far_planes_early.1.early = f32[3,2,4,304,128]{4,3,2,1,0:T(8,128)S(1)} custom-call(f32[21,2,8,128]{3,2,1,0:T(8,128)S(1)} %copy-done, f32[264,256]{1,0:T(8,128)S(1)} %constant_dynamic-update-slice_fusion.t0, f32[264,256]{1,0:T(8,128)S(1)} %collective-permute-done.5.t1, f32[264,256]{1,0:T(8,128)S(1)} %collective-permute-done.6.t2, ...), custom_call_target="tpu_custom_call" | custom-call | flops 34078720 | bytes 2621440 | tf_op jit(solution)/shard_map/far_planes_early/pallas_call | solution.py:303
  63.5 0.0 collective-permute-done.4.last
  63.5 4.2 %far_planes.1 = (f32[2,256,256]{2,1,0:T(8,128)}, f32[4,256,256]{2,1,0:T(8,128)}) custom-call(s32[2]{0:T(128)S(1)} %compare_select_fusion.scalar_ref, f32[21,2,8,128]{3,2,1,0:T(8,128)S(1)} %copy-done, f32[264,256]{1,0:T(8,128)S(1)} %collective-permute-done.4.last, f32[3,2,4,304,128]{4,3,2,1,0:T(8,128)S(1)} %far_planes_early.1.early, ...), custom_call_target="tpu_custom_call" | custom-call | flops 68157440 | bytes 2621440 | tf_op jit(solution)/shard_map/far_planes/pallas_call | solution.py:313
  (5 shorter events, 0.1 us)
Async XLA Ops:
  0.6 27.2 %collective-permute-start.7 = (f32[256,256]{1,0:T(8,128)}, f32[256,256]{1,0:T(8,128)S(1)}, u32[]{:S(2)}, u32[]{:S(2)}) collective-permute-start(f32[256,256]{1,0:T(8,128)} %bitcast.4), channel_id=1, source_target_pairs={{128,0},{129,1},{130,2},{131,3},{136,8},{137,9},{138,10},{139,11},... | collective-permute-start | bytes 786440 | tf_op jit(solution)/shard_map/ppermute | solution.py:29
  11.3 32.0 %collective-permute-start = (f32[256,256]{1,0:T(8,128)}, f32[256,256]{1,0:T(8,128)S(1)}, u32[]{:S(2)}, u32[]{:S(2)}) collective-permute-start(f32[256,256]{1,0:T(8,128)} %bitcast.5), channel_id=1, source_target_pairs={{132,0},{133,1},{134,2},{135,3},{140,8},{141,9},{142,10},{143,11},... | collective-permute-start | bytes 786440 | tf_op jit(solution)/shard_map/ppermute | solution.py:29
  15.1 7.2 %collective-permute-start.1 = (f32[4,256]{1,0:T(4,128)}, f32[4,256]{1,0:T(4,128)S(1)}, u32[]{:S(2)}, u32[]{:S(2)}) collective-permute-start(f32[4,256]{1,0:T(4,128)} %get-tuple-element.8), channel_id=1, source_target_pairs={{120,0},{121,1},{122,2},{123,3},{128,8},{129,9},{130,10},{131,11},... | collective-permute-start | bytes 12296 | tf_op jit(solution)/shard_map/ppermute | solution.py:29
  20.3 7.5 %collective-permute-start.2 = (f32[4,256]{1,0:T(4,128)}, f32[4,256]{1,0:T(4,128)S(1)}, u32[]{:S(2)}, u32[]{:S(2)}) collective-permute-start(f32[4,256]{1,0:T(4,128)} %get-tuple-element.9), channel_id=1, source_target_pairs={{136,0},{137,1},{138,2},{139,3},{144,8},{145,9},{146,10},{147,11},... | collective-permute-start | bytes 12296 | tf_op jit(solution)/shard_map/ppermute | solution.py:29
  27.9 21.9 %collective-permute-start.10 = (f32[264,256]{1,0:T(8,128)S(1)}, f32[264,256]{1,0:T(8,128)S(1)}, u32[]{:S(2)}, u32[]{:S(2)}) collective-permute-start(f32[264,256]{1,0:T(8,128)S(1)} %pad_maximum_fusion.t0), channel_id=1, source_target_pairs={{2,0},{3,1},{0,2},{1,3},{6,4},{7,5},{4,6},{5,7},{10,8},{11,9},{8,1... | collective-permute-start | bytes 811016 | tf_op jit(solution)/shard_map/ppermute | solution.py:41
  30.9 12.3 %collective-permute-start.3 = (f32[8,256]{1,0:T(8,128)S(1)}, f32[8,256]{1,0:T(8,128)S(1)}, u32[]{:S(2)}, u32[]{:S(2)}) collective-permute-start(f32[8,256]{1,0:T(8,128)S(1)} %pad_maximum_fusion.1), channel_id=1, source_target_pairs={{0,4},{1,5},{2,6},{3,7},{4,0},{5,1},{6,2},{7,3},{8,12},{9,13},{10,... | collective-permute-start | bytes 24584 | tf_op jit(solution)/shard_map/ppermute | solution.py:34
  37.6 14.8 %collective-permute-start.9 = (f32[264,256]{1,0:T(8,128)S(1)}, f32[264,256]{1,0:T(8,128)S(1)}, u32[]{:S(2)}, u32[]{:S(2)}) collective-permute-start(f32[264,256]{1,0:T(8,128)S(1)} %pad_maximum_fusion.t0), channel_id=1, source_target_pairs={{3,0},{0,1},{1,2},{2,3},{7,4},{4,5},{5,6},{6,7},{11,8},{8,9},{9,10... | collective-permute-start | bytes 811016 | tf_op jit(solution)/shard_map/ppermute | solution.py:41
  41.3 15.9 %collective-permute-start.8 = (f32[264,256]{1,0:T(8,128)S(1)}, f32[264,256]{1,0:T(8,128)S(1)}, u32[]{:S(2)}, u32[]{:S(2)}) collective-permute-start(f32[264,256]{1,0:T(8,128)S(1)} %pad_maximum_fusion.t0), channel_id=1, source_target_pairs={{1,0},{2,1},{3,2},{0,3},{5,4},{6,5},{7,6},{4,7},{9,8},{10,9},{11,1... | collective-permute-start | bytes 811016 | tf_op jit(solution)/shard_map/ppermute | solution.py:41
  43.3 18.5 %collective-permute-start.6 = (f32[264,256]{1,0:T(8,128)S(1)}, f32[264,256]{1,0:T(8,128)S(1)}, u32[]{:S(2)}, u32[]{:S(2)}) collective-permute-start(f32[264,256]{1,0:T(8,128)S(1)} %constant_dynamic-update-slice_fusion.t0), channel_id=1, source_target_pairs={{2,0},{3,1},{0,2},{1,3},{6,4},{7,5},{4,6},{5,7},{10,8},{11,9},{8,1... | collective-permute-start | bytes 811016 | tf_op jit(solution)/shard_map/ppermute | solution.py:41
  46.7 15.1 %collective-permute-start.5 = (f32[264,256]{1,0:T(8,128)S(1)}, f32[264,256]{1,0:T(8,128)S(1)}, u32[]{:S(2)}, u32[]{:S(2)}) collective-permute-start(f32[264,256]{1,0:T(8,128)S(1)} %constant_dynamic-update-slice_fusion.t0), channel_id=1, source_target_pairs={{3,0},{0,1},{1,2},{2,3},{7,4},{4,5},{5,6},{6,7},{11,8},{8,9},{9,10... | collective-permute-start | bytes 811016 | tf_op jit(solution)/shard_map/ppermute | solution.py:41
  49.8 13.6 %collective-permute-start.4 = (f32[264,256]{1,0:T(8,128)S(1)}, f32[264,256]{1,0:T(8,128)S(1)}, u32[]{:S(2)}, u32[]{:S(2)}) collective-permute-start(f32[264,256]{1,0:T(8,128)S(1)} %constant_dynamic-update-slice_fusion.t0), channel_id=1, source_target_pairs={{1,0},{2,1},{3,2},{0,3},{5,4},{6,5},{7,6},{4,7},{9,8},{10,9},{11,1... | collective-permute-start | bytes 811016 | tf_op jit(solution)/shard_map/ppermute | solution.py:41
  57.2 0.9 %copy-start = (f32[21,2,8,128]{3,2,1,0:T(8,128)S(1)}, f32[21,2,8,128]{3,2,1,0:T(8,128)}, u32[]{:S(2)}) copy-start(f32[21,2,8,128]{3,2,1,0:T(8,128)} %get-tuple-element.7.tables) | copy-start | bytes 516100

commit v5 on v3

--- a/solution.py
+++ b/solution.py
@@ -273,7 +273,8 @@
     near = jnp.concatenate([near, strips])
     near_tiles = [near] + [x_move(near, ahead) for ahead in NEAR[1:]]
     far = jnp.concatenate([far, swap(strips)])
-    far_tiles = [far] + [x_move(far, ahead) for ahead in FAR[1:]]
+    across, far = lax.optimization_barrier((near_tiles[NEAR.index(2)], far))
+    far_tiles = [far] + [swap(across) if ahead == 2 else x_move(far, ahead) for ahead in FAR[1:]]
 
     params = pltpu.CompilerParams(vmem_limit_bytes=24 << 20)
     state_shape = (6, 2, width, rows // 2)

time: 68.2 us -> 68.4 us (level)
  the two profiles are of different devices: /device:TPU:31 before, /device:TPU:158 now
where the time goes in v5:
time: 68.4 us; the launch traced here: 68 us
  starting transfers between devices  40.7 us (60%)
  waiting for transfers between devices  14 us (20%)
  Pallas kernels  11.4 us (17%)
  local copies, waits for them, and re-layouts  0.91 us (1%)
  between operations  0.9 us (1%)
    ppermute x4, starting transfers between devices, z_move(): return lax.ppermute(value, ('lon', 'plane'), pairs)  16.6 us
    ppermute x5, starting transfers between devices, x_move(): return lax.ppermute(value, 'plane', pairs)  15.1 us
    ppermute x2, waiting for transfers between devices, swap(): return lax.ppermute(value, 'plane', pairs)  14 us
    ppermute x2, starting transfers between devices, swap(): return lax.ppermute(value, 'plane', pairs)  8.99 us
    pallas_call x1, Pallas kernels, per_device(): pl.pallas_call(far_kernel, out_shape=(jax.ShapeDtypeStruct((2, rows, widt...  4.24 us
    pallas_call x1, Pallas kernels, per_device(): pl.pallas_call(near_kernel, out_shape=jax.ShapeDtypeStruct(state_shape, j...  3.68 us
    pallas_call x1, Pallas kernels, prepare(): pl.pallas_call(prepare_kernel, out_shape=(jax.ShapeDtypeStruct((HALO, row...  1.85 us
    pallas_call x1, Pallas kernels, per_device(): pl.pallas_call(early_kernel, out_shape=jax.ShapeDtypeStruct(fields_shape(...  1.62 us
  transfers between devices with their start and end apart: 11, of which 2 were waited for; matrix products, arithmetic and copies ran while one was open for 0% of the time, Pallas kernels for 11%

profile of v5, /device:TPU:158, one launch (start us, length us, event | category | flops | bytes accessed | tf_op | source)
XLA Modules:
  0.0 68.0 jit_solution(1153481333850902052)
XLA Ops:
  0.6 1.9 %collective-permute-start = (f32[256,256]{1,0:T(8,128)}, f32[256,256]{1,0:T(8,128)S(1)}, u32[]{:S(2)}, u32[]{:S(2)}) collective-permute-start(f32[256,256]{1,0:T(8,128)} %bitcast.4), channel_id=1, source_target_pairs={{128,0},{129,1},{130,2},{131,3},{136,8},{137,9},{138,10},{139,11},... | collective-permute-start | bytes 786440 | tf_op jit(solution)/shard_map/ppermute | solution.py:29
  2.6 1.8 %prepare.1 = (f32[4,256]{1,0:T(4,128)}, f32[4,256]{1,0:T(4,128)}, f32[21,2,8,128]{3,2,1,0:T(8,128)}) custom-call(f32[256,256]{1,0:T(8,128)} %bitcast.5, s32[2,256]{1,0:T(2,128)} %shift_ref.1, s32[2,256]{1,0:T(2,128)} %weight_ref.1, f32[1,256]{1,0:T(1,128)} %bitcast.7, f32[1,8]{1,0:T(1,128)} %gain_ref.1), custom_call_target="tpu_custom_call" | custom-call | flops 65536 | bytes 1048576 | tf_op jit(solution)/shard_map/prepare/pallas_call | solution.py:249
  4.4 1.9 %collective-permute-start.1 = (f32[4,256]{1,0:T(4,128)}, f32[4,256]{1,0:T(4,128)S(1)}, u32[]{:S(2)}, u32[]{:S(2)}) collective-permute-start(f32[4,256]{1,0:T(4,128)} %get-tuple-element.10), channel_id=1, source_target_pairs={{120,0},{121,1},{122,2},{123,3},{128,8},{129,9},{130,10},{131,11},... | collective-permute-start | bytes 12296 | tf_op jit(solution)/shard_map/ppermute | solution.py:29
  6.3 10.8 %collective-permute-start.2 = (f32[4,256]{1,0:T(4,128)}, f32[4,256]{1,0:T(4,128)S(1)}, u32[]{:S(2)}, u32[]{:S(2)}) collective-permute-start(f32[4,256]{1,0:T(4,128)} %get-tuple-element.11), channel_id=1, source_target_pairs={{136,0},{137,1},{138,2},{139,3},{144,8},{145,9},{146,10},{147,11},... | collective-permute-start | bytes 12296 | tf_op jit(solution)/shard_map/ppermute | solution.py:29
  17.2 1.9 %collective-permute-start.4 = (f32[256,256]{1,0:T(8,128)}, f32[256,256]{1,0:T(8,128)S(1)}, u32[]{:S(2)}, u32[]{:S(2)}) collective-permute-start(f32[256,256]{1,0:T(8,128)} %bitcast.6), channel_id=1, source_target_pairs={{132,0},{133,1},{134,2},{135,3},{140,8},{141,9},{142,10},{143,11},... | collective-permute-start | bytes 786440 | tf_op jit(solution)/shard_map/ppermute | solution.py:29
  19.1 0.0 collective-permute-done.1
  19.1 0.0 collective-permute-done.2
  19.1 0.0 collective-permute-done
  19.2 3.3 %collective-permute-start.3 = (f32[264,256]{1,0:T(8,128)S(1)}, f32[264,256]{1,0:T(8,128)S(1)}, u32[]{:S(2)}, u32[]{:S(2)}) collective-permute-start(f32[264,256]{1,0:T(8,128)S(1)} %pad_maximum_fusion.t0), channel_id=1, source_target_pairs={{2,0},{3,1},{0,2},{1,3},{6,4},{7,5},{4,6},{5,7},{10,8},{11,9},{8,1... | collective-permute-start | bytes 811016 | tf_op jit(solution)/shard_map/ppermute | solution.py:41
  22.5 6.9 %collective-permute-start.5 = (f32[8,256]{1,0:T(8,128)S(1)}, f32[8,256]{1,0:T(8,128)S(1)}, u32[]{:S(2)}, u32[]{:S(2)}) collective-permute-start(f32[8,256]{1,0:T(8,128)S(1)} %pad_maximum_fusion.2), channel_id=1, source_target_pairs={{0,4},{1,5},{2,6},{3,7},{4,0},{5,1},{6,2},{7,3},{8,12},{9,13},{10,... | collective-permute-start | bytes 24584 | tf_op jit(solution)/shard_map/ppermute | solution.py:34
  29.4 4.0 %collective-permute-start.10 = (f32[264,256]{1,0:T(8,128)S(1)}, f32[264,256]{1,0:T(8,128)S(1)}, u32[]{:S(2)}, u32[]{:S(2)}) collective-permute-start(f32[264,256]{1,0:T(8,128)S(1)} %pad_maximum_fusion.t0), channel_id=1, source_target_pairs={{3,0},{0,1},{1,2},{2,3},{7,4},{4,5},{5,6},{6,7},{11,8},{8,9},{9,10... | collective-permute-start | bytes 811016 | tf_op jit(solution)/shard_map/ppermute | solution.py:41
  33.5 1.9 %collective-permute-start.9 = (f32[264,256]{1,0:T(8,128)S(1)}, f32[264,256]{1,0:T(8,128)S(1)}, u32[]{:S(2)}, u32[]{:S(2)}) collective-permute-start(f32[264,256]{1,0:T(8,128)S(1)} %pad_maximum_fusion.t0), channel_id=1, source_target_pairs={{1,0},{2,1},{3,2},{0,3},{5,4},{6,5},{7,6},{4,7},{9,8},{10,9},{11,1... | collective-permute-start | bytes 811016 | tf_op jit(solution)/shard_map/ppermute | solution.py:41
  35.4 7.0 %collective-permute-done.5 = f32[8,256]{1,0:T(8,128)S(1)} collective-permute-done((f32[8,256]{1,0:T(8,128)S(1)}, f32[8,256]{1,0:T(8,128)S(1)}, u32[]{:S(2)}, u32[]{:S(2)}) %collective-permute-start.5) | collective-permute-done | bytes 8224 | tf_op jit(solution)/shard_map/ppermute | solution.py:34
  42.3 0.0 collective-permute-done.4
  42.4 0.0 collective-permute-done.3.t3
  42.4 2.1 %collective-permute-start.8 = (f32[264,256]{1,0:T(8,128)S(1)}, f32[264,256]{1,0:T(8,128)S(1)}, u32[]{:S(2)}, u32[]{:S(2)}) collective-permute-start(f32[264,256]{1,0:T(8,128)S(1)} %collective-permute-done.3.t3), channel_id=1, source_target_pairs={{0,4},{1,5},{2,6},{3,7},{4,0},{5,1},{6,2},{7,3},{8,12},{9,13},{10,... | collective-permute-start | bytes 811016 | tf_op jit(solution)/shard_map/ppermute | solution.py:34
  44.4 2.4 %collective-permute-start.7 = (f32[264,256]{1,0:T(8,128)S(1)}, f32[264,256]{1,0:T(8,128)S(1)}, u32[]{:S(2)}, u32[]{:S(2)}) collective-permute-start(f32[264,256]{1,0:T(8,128)S(1)} %pad_maximum_fusion.1.t0), channel_id=1, source_target_pairs={{3,0},{0,1},{1,2},{2,3},{7,4},{4,5},{5,6},{6,7},{11,8},{8,9},{9,10... | collective-permute-start | bytes 811016 | tf_op jit(solution)/shard_map/ppermute | solution.py:41
  46.8 3.5 %collective-permute-start.6 = (f32[264,256]{1,0:T(8,128)S(1)}, f32[264,256]{1,0:T(8,128)S(1)}, u32[]{:S(2)}, u32[]{:S(2)}) collective-permute-start(f32[264,256]{1,0:T(8,128)S(1)} %pad_maximum_fusion.1.t0), channel_id=1, source_target_pairs={{1,0},{2,1},{3,2},{0,3},{5,4},{6,5},{7,6},{4,7},{9,8},{10,9},{11,1... | collective-permute-start | bytes 811016 | tf_op jit(solution)/shard_map/ppermute | solution.py:41
  50.4 0.0 collective-permute-done.10.t2
  50.4 0.0 collective-permute-done.9.t1
  50.4 0.0 copy-start
  50.4 0.9 %copy-done = f32[21,2,8,128]{3,2,1,0:T(8,128)S(1)} copy-done((f32[21,2,8,128]{3,2,1,0:T(8,128)S(1)}, f32[21,2,8,128]{3,2,1,0:T(8,128)}, u32[]{:S(2)}) %copy-start) | copy-done | bytes 172056
  51.3 3.7 %near_planes.1.after.other = f32[6,2,256,128]{3,2,1,0:T(8,128)S(1)} custom-call(s32[2]{0:T(128)S(1)} %compare_select_fusion.scalar_ref, f32[21,2,8,128]{3,2,1,0:T(8,128)S(1)} %copy-done, f32[264,256]{1,0:T(8,128)S(1)} %pad_maximum_fusion.t0, f32[264,256]{1,0:T(8,128)S(1)} %collective-permute-done.9.t1, f32[264,256]{1,0:T(8,128)S(1)} %collective-permute-done.10.t2, ...), custom_call_target="tpu_custom_call" | custom-call | flops 68157440 | bytes 2621440 | tf_op jit(solution)/shard_map/near_planes/pallas_call | solution.py:281
  55.0 7.1 %collective-permute-done.8.t2 = f32[264,256]{1,0:T(8,128)S(1)} collective-permute-done((f32[264,256]{1,0:T(8,128)S(1)}, f32[264,256]{1,0:T(8,128)S(1)}, u32[]{:S(2)}, u32[]{:S(2)}) %collective-permute-start.8) | collective-permute-done | bytes 270368 | tf_op jit(solution)/shard_map/ppermute | solution.py:34
  62.1 0.0 collective-permute-done.7.t1
  62.1 1.6 %far_planes_early.1.early = f32[3,2,4,304,128]{4,3,2,1,0:T(8,128)S(1)} custom-call(f32[21,2,8,128]{3,2,1,0:T(8,128)S(1)} %copy-done, f32[264,256]{1,0:T(8,128)S(1)} %pad_maximum_fusion.1.t0, f32[264,256]{1,0:T(8,128)S(1)} %collective-permute-done.7.t1, f32[264,256]{1,0:T(8,128)S(1)} %collective-permute-done.8.t2, f32[6,2,256,128]{3,2,1,0:T(8,128)S(1)} %near_planes.1.after.other), custom_call_target="tpu_custom_call" | custom-call | flops 34078720 | bytes 2621440 | tf_op jit(solution)/shard_map/far_planes_early/pallas_call | solution.py:294
  63.7 0.0 collective-permute-done.6.last
  63.7 4.2 %far_planes.1 = (f32[2,256,256]{2,1,0:T(8,128)}, f32[4,256,256]{2,1,0:T(8,128)}) custom-call(s32[2]{0:T(128)S(1)} %compare_select_fusion.scalar_ref, f32[21,2,8,128]{3,2,1,0:T(8,128)S(1)} %copy-done, f32[264,256]{1,0:T(8,128)S(1)} %collective-permute-done.6.last, f32[3,2,4,304,128]{4,3,2,1,0:T(8,128)S(1)} %far_planes_early.1.early, ...), custom_call_target="tpu_custom_call" | custom-call | flops 68157440 | bytes 2621440 | tf_op jit(solution)/shard_map/far_planes/pallas_call | solution.py:304
  (4 shorter events, 0.1 us)
Async XLA Ops:
  0.6 18.5 %collective-permute-start = (f32[256,256]{1,0:T(8,128)}, f32[256,256]{1,0:T(8,128)S(1)}, u32[]{:S(2)}, u32[]{:S(2)}) collective-permute-start(f32[256,256]{1,0:T(8,128)} %bitcast.4), channel_id=1, source_target_pairs={{128,0},{129,1},{130,2},{131,3},{136,8},{137,9},{138,10},{139,11},... | collective-permute-start | bytes 786440 | tf_op jit(solution)/shard_map/ppermute | solution.py:29
  4.4 14.7 %collective-permute-start.1 = (f32[4,256]{1,0:T(4,128)}, f32[4,256]{1,0:T(4,128)S(1)}, u32[]{:S(2)}, u32[]{:S(2)}) collective-permute-start(f32[4,256]{1,0:T(4,128)} %get-tuple-element.10), channel_id=1, source_target_pairs={{120,0},{121,1},{122,2},{123,3},{128,8},{129,9},{130,10},{131,11},... | collective-permute-start | bytes 12296 | tf_op jit(solution)/shard_map/ppermute | solution.py:29
  6.3 12.8 %collective-permute-start.2 = (f32[4,256]{1,0:T(4,128)}, f32[4,256]{1,0:T(4,128)S(1)}, u32[]{:S(2)}, u32[]{:S(2)}) collective-permute-start(f32[4,256]{1,0:T(4,128)} %get-tuple-element.11), channel_id=1, source_target_pairs={{136,0},{137,1},{138,2},{139,3},{144,8},{145,9},{146,10},{147,11},... | collective-permute-start | bytes 12296 | tf_op jit(solution)/shard_map/ppermute | solution.py:29
  17.2 25.1 %collective-permute-start.4 = (f32[256,256]{1,0:T(8,128)}, f32[256,256]{1,0:T(8,128)S(1)}, u32[]{:S(2)}, u32[]{:S(2)}) collective-permute-start(f32[256,256]{1,0:T(8,128)} %bitcast.6), channel_id=1, source_target_pairs={{132,0},{133,1},{134,2},{135,3},{140,8},{141,9},{142,10},{143,11},... | collective-permute-start | bytes 786440 | tf_op jit(solution)/shard_map/ppermute | solution.py:29
  19.2 23.2 %collective-permute-start.3 = (f32[264,256]{1,0:T(8,128)S(1)}, f32[264,256]{1,0:T(8,128)S(1)}, u32[]{:S(2)}, u32[]{:S(2)}) collective-permute-start(f32[264,256]{1,0:T(8,128)S(1)} %pad_maximum_fusion.t0), channel_id=1, source_target_pairs={{2,0},{3,1},{0,2},{1,3},{6,4},{7,5},{4,6},{5,7},{10,8},{11,9},{8,1... | collective-permute-start | bytes 811016 | tf_op jit(solution)/shard_map/ppermute | solution.py:41
  22.5 19.8 %collective-permute-start.5 = (f32[8,256]{1,0:T(8,128)S(1)}, f32[8,256]{1,0:T(8,128)S(1)}, u32[]{:S(2)}, u32[]{:S(2)}) collective-permute-start(f32[8,256]{1,0:T(8,128)S(1)} %pad_maximum_fusion.2), channel_id=1, source_target_pairs={{0,4},{1,5},{2,6},{3,7},{4,0},{5,1},{6,2},{7,3},{8,12},{9,13},{10,... | collective-permute-start | bytes 24584 | tf_op jit(solution)/shard_map/ppermute | solution.py:34
  29.4 20.9 %collective-permute-start.10 = (f32[264,256]{1,0:T(8,128)S(1)}, f32[264,256]{1,0:T(8,128)S(1)}, u32[]{:S(2)}, u32[]{:S(2)}) collective-permute-start(f32[264,256]{1,0:T(8,128)S(1)} %pad_maximum_fusion.t0), channel_id=1, source_target_pairs={{3,0},{0,1},{1,2},{2,3},{7,4},{4,5},{5,6},{6,7},{11,8},{8,9},{9,10... | collective-permute-start | bytes 811016 | tf_op jit(solution)/shard_map/ppermute | solution.py:41
  33.5 16.9 %collective-permute-start.9 = (f32[264,256]{1,0:T(8,128)S(1)}, f32[264,256]{1,0:T(8,128)S(1)}, u32[]{:S(2)}, u32[]{:S(2)}) collective-permute-start(f32[264,256]{1,0:T(8,128)S(1)} %pad_maximum_fusion.t0), channel_id=1, source_target_pairs={{1,0},{2,1},{3,2},{0,3},{5,4},{6,5},{7,6},{4,7},{9,8},{10,9},{11,1... | collective-permute-start | bytes 811016 | tf_op jit(solution)/shard_map/ppermute | solution.py:41
  42.4 19.7 %collective-permute-start.8 = (f32[264,256]{1,0:T(8,128)S(1)}, f32[264,256]{1,0:T(8,128)S(1)}, u32[]{:S(2)}, u32[]{:S(2)}) collective-permute-start(f32[264,256]{1,0:T(8,128)S(1)} %collective-permute-done.3.t3), channel_id=1, source_target_pairs={{0,4},{1,5},{2,6},{3,7},{4,0},{5,1},{6,2},{7,3},{8,12},{9,13},{10,... | collective-permute-start | bytes 811016 | tf_op jit(solution)/shard_map/ppermute | solution.py:34
  44.4 17.6 %collective-permute-start.7 = (f32[264,256]{1,0:T(8,128)S(1)}, f32[264,256]{1,0:T(8,128)S(1)}, u32[]{:S(2)}, u32[]{:S(2)}) collective-permute-start(f32[264,256]{1,0:T(8,128)S(1)} %pad_maximum_fusion.1.t0), channel_id=1, source_target_pairs={{3,0},{0,1},{1,2},{2,3},{7,4},{4,5},{5,6},{6,7},{11,8},{8,9},{9,10... | collective-permute-start | bytes 811016 | tf_op jit(solution)/shard_map/ppermute | solution.py:41
  46.8 16.9 %collective-permute-start.6 = (f32[264,256]{1,0:T(8,128)S(1)}, f32[264,256]{1,0:T(8,128)S(1)}, u32[]{:S(2)}, u32[]{:S(2)}) collective-permute-start(f32[264,256]{1,0:T(8,128)S(1)} %pad_maximum_fusion.1.t0), channel_id=1, source_target_pairs={{1,0},{2,1},{3,2},{0,3},{5,4},{6,5},{7,6},{4,7},{9,8},{10,9},{11,1... | collective-permute-start | bytes 811016 | tf_op jit(solution)/shard_map/ppermute | solution.py:41
  50.4 0.9 %copy-start = (f32[21,2,8,128]{3,2,1,0:T(8,128)S(1)}, f32[21,2,8,128]{3,2,1,0:T(8,128)}, u32[]{:S(2)}) copy-start(f32[21,2,8,128]{3,2,1,0:T(8,128)} %get-tuple-element.9.tables) | copy-start | bytes 516100
